TPU v7x, 32 devices: a whole 2x2x4 slice. The times are simulated.
32 devices in a mesh: shard: 4 (over y, x), replica: 8 (over z, core).
Axes of the slice: x: 2, y: 2, z: 4, core: 2. Of those that a mesh axis runs over, the one named last changes fastest.
Arguments:
- series: bfloat16 [128, 16384], P(('shard', 'replica')), may hold values from -6 to 6
- mask: int32 [128, 256], P(('shard', 'replica')), may hold values from 0 to 1, as said below
- qkv_w: float32 [2, 512, 1536], P(None, 'shard'), may hold values from -0.25 to 0.25
- out_w: float32 [2, 512, 512], P(None, 'shard'), may hold values from -1 to 1
- up_w: float32 [2, 512, 2048], P(None, 'shard'), may hold values from -0.25 to 0.25
- down_w: float32 [2, 2048, 512], P(None, 'shard'), may hold values from -0.125 to 0.125
- patch_maps: float32 [384, 512], P(None, 'shard')
- norm_params: float32 [10, 512], P(None, 'shard')
- qkv_m: float32 [2, 512, 1536], P(None, 'shard'), may hold values from -5.9604645e-07 to 5.9604645e-07
- out_m: float32 [2, 512, 512], P(None, 'shard'), may hold values from -5.9604645e-07 to 5.9604645e-07
- up_m: float32 [2, 512, 2048], P(None, 'shard'), may hold values from -5.9604645e-07 to 5.9604645e-07
- down_m: float32 [2, 2048, 512], P(None, 'shard'), may hold values from -5.9604645e-07 to 5.9604645e-07
- patch_m: float32 [384, 512], P(None, 'shard'), may hold values from -5.9604645e-07 to 5.9604645e-07
- norm_m: float32 [10, 512], P(None, 'shard'), may hold values from -3.33786e-06 to 3.33786e-06
- qkv_v: float32 [2, 512, 1536], P(None, 'shard'), may hold values from 7.7003825e-17 to 1.2320612e-15
- out_v: float32 [2, 512, 512], P(None, 'shard'), may hold values from 7.7003825e-17 to 1.2320612e-15
- up_v: float32 [2, 512, 2048], P(None, 'shard'), may hold values from 7.7003825e-17 to 1.2320612e-15
- down_v: float32 [2, 2048, 512], P(None, 'shard'), may hold values from 7.7003825e-17 to 1.2320612e-15
- patch_v: float32 [384, 512], P(None, 'shard'), may hold values from 7.7003825e-17 to 1.2320612e-15
- norm_v: float32 [10, 512], P(None, 'shard'), may hold values from 1.9250956e-15 to 3.080153e-14
Outputs:
- loss: float32 [], replicated
- grad_norm: float32 [], replicated
- qkv_new: float32 [2, 512, 1536], P(None, 'shard')
- out_new: float32 [2, 512, 512], P(None, 'shard')
- up_new: float32 [2, 512, 2048], P(None, 'shard')
- down_new: float32 [2, 2048, 512], P(None, 'shard')
- patch_new: float32 [384, 512], P(None, 'shard')
- norm_new: float32 [10, 512], P(None, 'shard')
- qkv_m_new: float32 [2, 512, 1536], P(None, 'shard')
- out_m_new: float32 [2, 512, 512], P(None, 'shard')
- up_m_new: float32 [2, 512, 2048], P(None, 'shard')
- down_m_new: float32 [2, 2048, 512], P(None, 'shard')
- patch_m_new: float32 [384, 512], P(None, 'shard')
- norm_m_new: float32 [10, 512], P(None, 'shard')
- qkv_v_new: float32 [2, 512, 1536], P(None, 'shard')
- out_v_new: float32 [2, 512, 512], P(None, 'shard')
- up_v_new: float32 [2, 512, 2048], P(None, 'shard')
- down_v_new: float32 [2, 2048, 512], P(None, 'shard')
- patch_v_new: float32 [384, 512], P(None, 'shard')
- norm_v_new: float32 [10, 512], P(None, 'shard')
Inputs may be any that keep to these rules, and one draw needn't show every extreme that they name: `mask`: each series has exactly 102 masked patches.
All inputs are finite; a program needn't handle non-finite values.
Results may differ from a plain program's by a relative error of at most 0.02.
Values may be sent and summed in bfloat16 or wider, within the bound.
No kernel may reach another device: no remote copies, remote signals or barrier semaphores. Data moves between devices by JAX's collectives and lax.ppermute only.
A program may use at most 256 MiB of HBM per device.

v0:
```python
import jax
import jax.numpy as jnp
from jax import lax
from jax.sharding import PartitionSpec as P

D = 512
H = 8
DH = 64
P_SIZE = 64
LEN = 256
L = 2
MASKED = 102


EPS = 1e-05
CLIP = 0.001
RATE = 0.05
TABLE_RATE = 0.3
BETA_ONE = 0.9
BETA_TWO = 0.999
ADAM_EPS = 1e-08
DECAY = 0.1
STEP_COUNT = 10


def as_sent(x):

    def short(part):
        return part.astype(jnp.bfloat16) if part.dtype == jnp.float32 else part

    return jax.tree.map(short, x)


def layer_norm(x, gain, bias):
    center = x - jnp.mean(x, -1, keepdims=True)
    spread = jnp.mean(center * center, -1, keepdims=True)
    return center * lax.rsqrt(spread + EPS) * gain + bias


def dense(left, right):
    return jnp.dot(left, right, preferred_element_type=jnp.float32)


def dense_tn(left, right):
    return lax.dot_general(
        left, right, (((0,), (0,)), ((), ())), preferred_element_type=jnp.float32
    )


def dense_nt(left, right):
    return lax.dot_general(
        left, right, (((1,), (1,)), ((), ())), preferred_element_type=jnp.float32
    )


def gather_layer(stack, index):
    pieces = tuple((w[index].astype(jnp.bfloat16) for w in stack))
    return (
        lax.all_gather(pieces[0], "shard", axis=0, tiled=True),
        lax.all_gather(pieces[1], "shard", axis=0, tiled=True),
        lax.all_gather(pieces[2], "shard", axis=0, tiled=True),
        lax.all_gather(pieces[3], "shard", axis=0, tiled=True),
    )


def layer_forward(x, weights, norms, seqs):
    w_qkv, w_out, w_up, w_down = weights
    rows = x.shape[0]
    normed_a = layer_norm(x, norms[0], norms[1]).astype(jnp.bfloat16)
    qkv = dense(normed_a, w_qkv).astype(jnp.bfloat16).reshape(seqs, LEN, 3, H, DH)
    query, key, value = (qkv[:, :, 0], qkv[:, :, 1], qkv[:, :, 2])
    scores = jnp.einsum("sqhd,skhd->shqk", query, key, preferred_element_type=jnp.float32) * DH ** (
        -0.5
    )
    probs = jax.nn.softmax(scores, axis=-1)
    probs_low = probs.astype(jnp.bfloat16)
    attended = jnp.einsum("shqk,skhd->sqhd", probs_low, value, preferred_element_type=jnp.float32)
    attended = attended.astype(jnp.bfloat16).reshape(rows, D)
    mid = x + dense(attended, w_out)
    normed_b = layer_norm(mid, norms[2], norms[3]).astype(jnp.bfloat16)
    upper = dense(normed_b, w_up)
    active = jax.nn.gelu(upper, approximate=False).astype(jnp.bfloat16)
    result = mid + dense(active, w_down)
    saved = (normed_a, query, key, value, probs, probs_low, attended, mid, normed_b, upper, active)
    return (result, saved)


def layer_backward(x, grad_out, weights, norms, seqs):
    w_qkv, w_out, w_up, w_down = weights
    rows = x.shape[0]
    _, saved = layer_forward(x, weights, norms, seqs)
    normed_a, query, key, value, probs, probs_low, attended, mid, normed_b, upper, active = saved
    grad_low = grad_out.astype(jnp.bfloat16)
    g_down = dense_tn(active, grad_low)
    grad_active = dense_nt(grad_low, w_down)
    _, gelu_back = jax.vjp(lambda v: jax.nn.gelu(v, approximate=False), upper)
    grad_upper = gelu_back(grad_active)[0].astype(jnp.bfloat16)
    g_up = dense_tn(normed_b, grad_upper)
    _, norm_back_b = jax.vjp(layer_norm, mid, norms[2], norms[3])
    grad_mid_n, gain_b, bias_b = norm_back_b(dense_nt(grad_upper, w_up))
    grad_mid = grad_out + grad_mid_n
    grad_mid_low = grad_mid.astype(jnp.bfloat16)
    g_out = dense_tn(attended, grad_mid_low)
    grad_att = dense_nt(grad_mid_low, w_out).astype(jnp.bfloat16).reshape(seqs, LEN, H, DH)
    grad_probs = jnp.einsum("sqhd,skhd->shqk", grad_att, value, preferred_element_type=jnp.float32)
    grad_value = jnp.einsum(
        "shqk,sqhd->skhd", probs_low, grad_att, preferred_element_type=jnp.float32
    )
    grad_scores = probs * (grad_probs - jnp.sum(grad_probs * probs, -1, keepdims=True))
    grad_scores = grad_scores.astype(jnp.bfloat16)
    grad_query = jnp.einsum(
        "shqk,skhd->sqhd", grad_scores, key, preferred_element_type=jnp.float32
    ) * DH ** (-0.5)
    grad_key = jnp.einsum(
        "shqk,sqhd->skhd", grad_scores, query, preferred_element_type=jnp.float32
    ) * DH ** (-0.5)
    grad_qkv = (
        jnp.stack([grad_query, grad_key, grad_value], axis=2)
        .reshape(rows, 3 * D)
        .astype(jnp.bfloat16)
    )
    g_qkv = dense_tn(normed_a, grad_qkv)
    _, norm_back_a = jax.vjp(layer_norm, x, norms[0], norms[1])
    grad_x_n, gain_a, bias_a = norm_back_a(dense_nt(grad_qkv, w_qkv))
    norm_grads = jnp.stack([gain_a, bias_a, gain_b, bias_b])
    return (grad_mid + grad_x_n, (g_qkv, g_out, g_up, g_down), norm_grads)


def adam(weight, first, second, grad, rate):
    first = BETA_ONE * first + (1 - BETA_ONE) * grad
    second = BETA_TWO * second + (1 - BETA_TWO) * grad * grad
    fixed_one = first / (1 - BETA_ONE**STEP_COUNT)
    fixed_two = second / (1 - BETA_TWO**STEP_COUNT)
    weight = weight - rate * (fixed_one / (jnp.sqrt(fixed_two) + ADAM_EPS) + DECAY * weight)
    return (weight, first, second)


def on_device(
    series,
    mask,
    qkv_w,
    out_w,
    up_w,
    down_w,
    patch_maps,
    norm_params,
    qkv_m,
    out_m,
    up_m,
    down_m,
    patch_m,
    norm_m,
    qkv_v,
    out_v,
    up_v,
    down_v,
    patch_v,
    norm_v,
):
    seqs = series.shape[0]
    rows = seqs * LEN
    target = series.reshape(rows, P_SIZE).astype(jnp.float32)
    maskf = mask.reshape(rows, 1).astype(jnp.float32)
    inputs = (target * (1.0 - maskf)).astype(jnp.bfloat16)
    maps, norms_all = (
        lax.all_gather(patch_maps, "shard", axis=1, tiled=True),
        lax.all_gather(norm_params, "shard", axis=1, tiled=True),
    )
    embed = maps[:P_SIZE].astype(jnp.bfloat16)
    head = maps[P_SIZE : 2 * P_SIZE].astype(jnp.bfloat16)
    table = maps[2 * P_SIZE :]
    x = dense(inputs, embed) + jnp.tile(table, (seqs, 1))
    stack = (qkv_w, out_w, up_w, down_w)
    inputs_kept = []
    weights_kept = []
    for index in range(L):
        weights = gather_layer(stack, index)
        inputs_kept.append(x)
        weights_kept.append(weights)
        x, _ = layer_forward(x, weights, norms_all[4 * index : 4 * index + 4], seqs)
    final = layer_norm(x, norms_all[4 * L], norms_all[4 * L + 1])
    final_low = final.astype(jnp.bfloat16)
    pred = dense_nt(final_low, head)
    err = pred - target
    count = MASKED * seqs * lax.axis_size("shard") * lax.axis_size("replica")
    local_error = jnp.sum(maskf * jnp.mean(err * err, -1, keepdims=True))
    loss = lax.psum(local_error, ("shard", "replica")) / count
    grad_pred = (maskf * err * (2.0 / (P_SIZE * count))).astype(jnp.bfloat16)
    g_head = dense_tn(grad_pred, final_low)
    _, final_back = jax.vjp(layer_norm, x, norms_all[4 * L], norms_all[4 * L + 1])
    grad_x, gain_f, bias_f = final_back(dense(grad_pred, head))
    layer_grads = [None] * L
    norm_grads = [None] * L
    for index in reversed(range(L)):
        weights = gather_layer(stack, index)
        grad_x, grads, gnorms = layer_backward(
            inputs_kept[index], grad_x, weights, norms_all[4 * index : 4 * index + 4], seqs
        )
        owned = (
            lax.psum_scatter(
                grads[0].astype(jnp.bfloat16), "shard", scatter_dimension=0, tiled=True
            ).astype(jnp.float32),
            lax.psum_scatter(
                grads[1].astype(jnp.bfloat16), "shard", scatter_dimension=0, tiled=True
            ).astype(jnp.float32),
            lax.psum_scatter(
                grads[2].astype(jnp.bfloat16), "shard", scatter_dimension=0, tiled=True
            ).astype(jnp.float32),
            lax.psum_scatter(
                grads[3].astype(jnp.bfloat16), "shard", scatter_dimension=0, tiled=True
            ).astype(jnp.float32),
        )
        layer_grads[index] = owned
        norm_grads[index] = gnorms
    g_embed = dense_tn(inputs, grad_x.astype(jnp.bfloat16))
    g_table = jnp.sum(grad_x.reshape(seqs, LEN, D), 0)
    g_maps = jnp.concatenate([g_embed, g_head, g_table], 0)
    g_norms = jnp.concatenate(norm_grads + [jnp.stack([gain_f, bias_f])], 0)
    small = (
        lax.psum_scatter(
            g_maps.astype(jnp.bfloat16), "shard", scatter_dimension=1, tiled=True
        ).astype(jnp.float32),
        lax.psum_scatter(
            g_norms.astype(jnp.bfloat16), "shard", scatter_dimension=1, tiled=True
        ).astype(jnp.float32),
    )
    stacked = tuple((jnp.stack([layer_grads[i][j] for i in range(L)]) for j in range(4)))
    grads_all = jax.tree.map(
        lambda part: part.astype(jnp.float32), lax.psum(as_sent(stacked + small), "replica")
    )
    squares = jnp.zeros((), jnp.float32)
    for grad in grads_all:
        squares = squares + jnp.sum(grad * grad)
    grad_norm = jnp.sqrt(lax.psum(squares, "shard"))
    factor = CLIP / jnp.maximum(grad_norm, CLIP)
    params = (qkv_w, out_w, up_w, down_w, patch_maps, norm_params)
    firsts = (qkv_m, out_m, up_m, down_m, patch_m, norm_m)
    seconds = (qkv_v, out_v, up_v, down_v, patch_v, norm_v)
    rates = (RATE, RATE, RATE, RATE, TABLE_RATE, TABLE_RATE)
    results = [
        adam(w, m, v, g * factor, r)
        for w, m, v, g, r in zip(params, firsts, seconds, grads_all, rates)
    ]
    news = tuple((r[0] for r in results))
    new_m = tuple((r[1] for r in results))
    new_v = tuple((r[2] for r in results))
    return (
        loss,
        grad_norm,
        news[0],
        news[1],
        news[2],
        news[3],
        news[4],
        news[5],
        new_m[0],
        new_m[1],
        new_m[2],
        new_m[3],
        new_m[4],
        new_m[5],
        new_v[0],
        new_v[1],
        new_v[2],
        new_v[3],
        new_v[4],
        new_v[5],
    )


def solution(mesh):
    in_specs = (
        P(("shard", "replica"), None),
        P(("shard", "replica"), None),
        P(None, "shard", None),
        P(None, "shard", None),
        P(None, "shard", None),
        P(None, "shard", None),
        P(None, "shard"),
        P(None, "shard"),
        P(None, "shard", None),
        P(None, "shard", None),
        P(None, "shard", None),
        P(None, "shard", None),
        P(None, "shard"),
        P(None, "shard"),
        P(None, "shard", None),
        P(None, "shard", None),
        P(None, "shard", None),
        P(None, "shard", None),
        P(None, "shard"),
        P(None, "shard"),
    )
    out_specs = (
        P(),
        P(),
        P(None, "shard", None),
        P(None, "shard", None),
        P(None, "shard", None),
        P(None, "shard", None),
        P(None, "shard"),
        P(None, "shard"),
        P(None, "shard", None),
        P(None, "shard", None),
        P(None, "shard", None),
        P(None, "shard", None),
        P(None, "shard"),
        P(None, "shard"),
        P(None, "shard", None),
        P(None, "shard", None),
        P(None, "shard", None),
        P(None, "shard", None),
        P(None, "shard"),
        P(None, "shard"),
    )
    return jax.shard_map(
        on_device, mesh=mesh, in_specs=in_specs, out_specs=out_specs, check_vma=False
    )
```

profile of v0, /device:TPU:0, one launch (start us, length us, event | category | flops | bytes accessed | tf_op | source)
XLA Modules:
  0.0 814.6 jit_solution(3373705692409527471)
XLA Ops:
  15.0 20.9 %all_gather.38 = f32[384,512]{1,0:T(8,128)S(1)} all-gather(f32[384,128]{1,0:T(8,128)S(1)} %copy-done.62), channel_id=1, replica_groups=mesh['shard'=4,'replica'=8] {'shard'}, dimensions={1}, use_global_device_ids=true | all-gather | bytes 983040 | tf_op jit(solution)/shard_map/all_gather | solution.py:166
  36.8 8.7 %all_gather.39 = f32[10,512]{1,0:T(8,128)S(1)} all-gather(f32[10,128]{1,0:T(8,128)S(1)} %copy-done.91), channel_id=1, replica_groups=mesh['shard'=4,'replica'=8] {'shard'}, dimensions={1}, use_global_device_ids=true | all-gather | bytes 25600 | tf_op jit(solution)/shard_map/all_gather | solution.py:167
  46.2 9.8 %all-gather.5 = bf16[1,512,512]{2,1,0:T(8,128)(2,1)} all-gather(bf16[1,128,512]{2,1,0:T(8,128)(2,1)S(1)} %get-tuple-element.84), channel_id=7, replica_groups=mesh['shard'=4,'replica'=8] {'shard'}, dimensions={1}, use_global_device_ids=true | all-gather | bytes 655360 | tf_op jit(solution)/shard_map/all_gather | solution.py:60
  57.2 12.2 %all-gather.1 = bf16[1,512,512]{2,1,0:T(8,128)(2,1)} all-gather(bf16[1,128,512]{2,1,0:T(8,128)(2,1)S(1)} %get-tuple-element.85), channel_id=3, replica_groups=mesh['shard'=4,'replica'=8] {'shard'}, dimensions={1}, use_global_device_ids=true | all-gather | bytes 655360 | tf_op jit(solution)/shard_map/all_gather | solution.py:60
  73.2 5.2 convolution_convert_fusion.1
  78.4 9.0 %reshape.311 = bf16[4,256,3,8,64]{4,3,2,1,0:T(8,128)(2,1)} reshape(bf16[1024,1536]{1,0:T(8,128)(2,1)} %convolution_convert_fusion.1) | data formatting | bytes 6291456 | tf_op jit(solution)/shard_map/reshape | solution.py:70
  87.5 5.7 fusion.172
  93.2 3.0 copy.133
  96.2 3.1 copy.132
  99.3 3.0 copy.134
  102.3 2.8 fusion.108
  105.2 6.3 fusion.178
  119.2 24.3 %multiply_convert_fusion.3 = (bf16[1024,2048]{1,0:T(8,128)(2,1)}, f32[1024,2048]{1,0:T(8,128)}, f32[1024,2048]{1,0:T(8,128)}) fusion(bf16[1,512,2048]{2,1,0:T(8,128)(2,1)} %all-gather.17.cloned.1.call-done, f32[1024,512]{1,0:T(8,128)} %copy-done.14, f32[512]{0:T(512)S(1)} %bitcast.271, f32[512]{0:T(512)S(1)} %bitcast.257, f32[1024]{0:T(1024)S(1)} %fusion.144, ...), kind=kOutput, calls=%fused_computation.26 | convolution fusion | flops 2286419968 | bytes 25178112 | tf_op jit(solution)/shard_map/dot_general | solution.py:41
  143.6 6.1 fusion.180
  151.0 6.0 all-gather.21.cloned.1.call-done
  157.0 4.9 convolution_convert_fusion
  161.9 8.9 %reshape.312 = bf16[4,256,3,8,64]{4,3,2,1,0:T(8,128)(2,1)} reshape(bf16[1024,1536]{1,0:T(8,128)(2,1)} %convolution_convert_fusion) | data formatting | bytes 6291456 | tf_op jit(solution)/shard_map/reshape | solution.py:70
  170.8 5.7 fusion.171
  178.7 3.0 copy.135
  181.8 3.0 copy.137
  184.8 2.5 fusion.100
  187.3 6.3 fusion.181
  200.8 24.6 %multiply_convert_fusion.2 = (bf16[1024,2048]{1,0:T(8,128)(2,1)}, f32[1024,2048]{1,0:T(8,128)}, f32[1024,2048]{1,0:T(8,128)}) fusion(bf16[1,512,2048]{2,1,0:T(8,128)(2,1)} %all-gather.23.cloned.1.call-done, f32[1024,512]{1,0:T(8,128)} %copy-done.11, f32[512]{0:T(512)S(1)} %bitcast.273, f32[512]{0:T(512)S(1)} %bitcast.261, f32[1024]{0:T(1024)S(1)} %fusion.146, ...), kind=kOutput, calls=%fused_computation.12 | convolution fusion | flops 2286419968 | bytes 25178112 | tf_op jit(solution)/shard_map/dot_general | solution.py:41
  225.4 6.8 all-gather.25.cloned.1.call-done
  232.2 5.3 fusion.183
  241.7 2.6 multiply_reduce_fusion.4
  246.2 7.4 add_convert_fusion.1
  253.6 3.4 multiply_reduce_fusion.5
  260.6 3.9 reshape.313
  264.5 3.0 copy.99
  267.5 5.2 fusion.83
  272.7 5.0 multiply_reduce_fusion.1
  282.4 2.9 copy.104
  288.0 3.0 multiply_reduce_fusion.6
  294.2 8.7 %add_convert_fusion = bf16[1024,2048]{1,0:T(8,128)(2,1)S(1)} fusion(f32[1024,2048]{1,0:T(8,128)} %get-tuple-element.71, f32[1024,2048]{1,0:T(8,128)} %get-tuple-element.102, bf16[1,2048,512]{2,1,0:T(8,128)(2,1)S(1)} %copy-done.132, f32[1024,512]{1,0:T(8,128)S(1)} %add_add_fusion.7), kind=kOutput, calls=%fused_computation.8 | convolution fusion | flops 2177368064 | bytes 25165824 | tf_op jit(solution)/shard_map/dot_general | solution.py:51
  303.0 3.5 multiply_reduce_fusion.7
  314.2 4.9 fusion.89
  319.1 5.0 multiply_reduce_fusion
  328.7 2.9 copy.111
  334.9 3.1 multiply_reduce_fusion.8
  342.5 2.7 reduce_sum.428
  348.8 3.5 convolution_convert_fusion.11
  352.7 5.3 convolution_convert_fusion.6
  358.1 5.0 convolution_convert_fusion.7
  363.2 6.1 convolution_convert_fusion.4
  370.9 6.1 convolution_convert_fusion.5
  378.6 5.9 convolution_convert_fusion.2
  386.2 5.9 convolution_convert_fusion.3
  395.5 4.4 reduce-scatter.21.cloned.1.call-done
  399.9 28.4 %reduce-scatter.19.cloned.1.call-done = bf16[128,512]{1,0:T(8,128)(2,1)} async-done(((bf16[512,512]{1,0:T(8,128)(2,1)}), bf16[128,512]{1,0:T(8,128)(2,1)}) %reduce-scatter.19.cloned.1.call-update) | async-done | bytes 131088 | tf_op jit(solution)/shard_map/reduce_scatter | solution.py:203
  430.0 32.7 %reduce-scatter.17.cloned.1.call-done = bf16[128,1536]{1,0:T(8,128)(2,1)} async-done(((bf16[512,1536]{1,0:T(8,128)(2,1)}), bf16[128,1536]{1,0:T(8,128)(2,1)}) %reduce-scatter.17.cloned.1.call-update) | async-done | bytes 393232 | tf_op jit(solution)/shard_map/reduce_scatter | solution.py:200
  462.7 34.5 %reduce-scatter.15.cloned.1.call-done = bf16[128,1536]{1,0:T(8,128)(2,1)} async-done(((bf16[512,1536]{1,0:T(8,128)(2,1)}), bf16[128,1536]{1,0:T(8,128)(2,1)}) %reduce-scatter.15.cloned.1.call-update) | async-done | bytes 393232 | tf_op jit(solution)/shard_map/reduce_scatter | solution.py:200
  499.3 36.6 %reduce-scatter.25.cloned.1.call-done = bf16[128,2048]{1,0:T(8,128)(2,1)} async-done(((bf16[512,2048]{1,0:T(8,128)(2,1)}), bf16[128,2048]{1,0:T(8,128)(2,1)}) %reduce-scatter.25.cloned.1.call-update) | async-done | bytes 524304 | tf_op jit(solution)/shard_map/reduce_scatter | solution.py:206
  535.9 39.0 %reduce-scatter.23.cloned.1.call-done = bf16[128,2048]{1,0:T(8,128)(2,1)} async-done(((bf16[512,2048]{1,0:T(8,128)(2,1)}), bf16[128,2048]{1,0:T(8,128)(2,1)}) %reduce-scatter.23.cloned.1.call-update) | async-done | bytes 524304 | tf_op jit(solution)/shard_map/reduce_scatter | solution.py:206
  577.2 36.4 %reduce-scatter.29.cloned.1.call-done = bf16[512,512]{1,0:T(8,128)(2,1)} async-done(((bf16[2048,512]{1,0:T(8,128)(2,1)}), bf16[512,512]{1,0:T(8,128)(2,1)}) %reduce-scatter.29.cloned.1.call-update) | async-done | bytes 524304 | tf_op jit(solution)/shard_map/reduce_scatter | solution.py:209
  613.5 38.9 %reduce-scatter.27.cloned.1.call-done = bf16[512,512]{1,0:T(8,128)(2,1)} async-done(((bf16[2048,512]{1,0:T(8,128)(2,1)}), bf16[512,512]{1,0:T(8,128)(2,1)}) %reduce-scatter.27.cloned.1.call-update) | async-done | bytes 524304 | tf_op jit(solution)/shard_map/reduce_scatter | solution.py:209
  656.0 39.5 %psum.56 = f32[]{:T(128)} all-reduce(f32[]{:T(128)} %multiply_reduce_fusion.20), channel_id=1, replica_groups=mesh['shard'=4,'replica'=8] {'shard','replica'}, use_global_device_ids=true, to_apply=%region_16.0 | all-reduce | flops 1 | bytes 8 | tf_op jit(solution)/shard_map/psum | solution.py:187
  696.3 16.5 %psum.62 = bf16[10,128]{1,0:T(8,128)(2,1)S(1)} all-reduce(bf16[10,128]{1,0:T(8,128)(2,1)S(1)} %copy.123), channel_id=1, replica_groups=mesh['shard'=4,'replica'=8] {'replica'}, use_global_device_ids=true, to_apply=%region_60.0 | all-reduce | flops 1280 | bytes 5120 | tf_op jit(solution)/shard_map/psum | solution.py:229
  713.4 50.8 %all-reduce.3.cloned.1.call-done = (bf16[2,128,1536]{2,1,0:T(8,128)(2,1)}, bf16[2,128,512]{2,1,0:T(8,128)(2,1)}, bf16[2,128,2048]{2,1,0:T(8,128)(2,1)}, bf16[2,512,512]{2,1,0:T(8,128)(2,1)}, bf16[384,128]{1,0:T(8,128)(2,1)}) async-done(((bf16[2,128,1536]{2,1,0:T(8,128)(2,1)}, bf16[2,128,512]{2,1,0:T(8,128)(2,1)}, bf16[2,128,2048]{2,1,0:T(8,128)(2,1)}, bf16[2,512,512]{2,1,0:T(8,128)(2,1)}, ...) | async-done | bytes 3244048 | tf_op jit(solution)/shard_map/psum | solution.py:229
  765.9 2.5 fusion.27
  777.0 10.3 %psum.63 = f32[]{:T(128)} all-reduce(f32[]{:T(128)S(6)} %add.328), channel_id=1, replica_groups=mesh['shard'=4,'replica'=8] {'shard'}, use_global_device_ids=true, to_apply=%region_62.0 | all-reduce | flops 1 | bytes 8 | tf_op jit(solution)/shard_map/psum | solution.py:234
  791.2 3.1 multiply_subtract_fusion.2
  796.1 4.0 multiply_subtract_fusion
  801.5 3.9 multiply_subtract_fusion.1
  (439 shorter events, 107.2 us)
Async XLA Ops:
  7.2 66.0 %all-gather.15.cloned.1.call-start = ((), (), s32[]{:S(2)}) async-start(), calls=%async_computation.18 | async-start | bytes 1966080 | tf_op jit(solution)/shard_map/all_gather | solution.py:59
  9.8 109.4 %all-gather.17.cloned.1.call-start = ((), (), s32[]{:S(2)}) async-start(), calls=%async_computation.19 | async-start | bytes 2621440 | tf_op jit(solution)/shard_map/all_gather | solution.py:61
  11.1 132.4 %all-gather.19.cloned.1.call-start = ((), (), s32[]{:S(2)}) async-start(), calls=%async_computation.20 | async-start | bytes 2621440 | tf_op jit(solution)/shard_map/all_gather | solution.py:62
  13.2 143.8 %all-gather.21.cloned.1.call-start = ((), (), s32[]{:S(2)}) async-start(), calls=%async_computation.21 | async-start | bytes 1966080 | tf_op jit(solution)/shard_map/all_gather | solution.py:59
  13.8 187.0 %all-gather.23.cloned.1.call-start = ((), (), s32[]{:S(2)}) async-start(), calls=%async_computation.22 | async-start | bytes 2621440 | tf_op jit(solution)/shard_map/all_gather | solution.py:61
  13.8 22.2 %copy-start.94 = (s32[4,256]{1,0:T(4,128)S(1)}, s32[4,256]{1,0:T(4,128)}, u32[]{:S(2)}) copy-start(s32[4,256]{1,0:T(4,128)} %param.21) | copy-start | bytes 12292
  13.9 23.0 %copy-start.91 = (f32[10,128]{1,0:T(8,128)S(1)}, f32[10,128]{1,0:T(8,128)}, u32[]{:S(2)}) copy-start(f32[10,128]{1,0:T(8,128)} %param.27) | copy-start | bytes 15364
  13.9 32.2 %copy-start.44 = (f32[2,128,512]{2,1,0:T(8,128)S(1)}, f32[2,128,512]{2,1,0:T(8,128)}, u32[]{:S(2)}) copy-start(f32[2,128,512]{2,1,0:T(8,128)} %param.23) | copy-start | bytes 1572868
  14.4 217.8 %all-gather.25.cloned.1.call-start = ((), (), s32[]{:S(2)}) async-start(), calls=%async_computation.23 | async-start | bytes 2621440 | tf_op jit(solution)/shard_map/all_gather | solution.py:62
  15.0 378.9 %reduce-scatter.31.cloned.1.call-start = ((), (), s32[]{:S(2)}) async-start(), calls=%async_computation.24 | async-start | bytes 491520
  36.0 20.0 %copy-start.71 = (bf16[4,16384]{1,0:T(4,128)(2,1)S(1)}, bf16[4,16384]{1,0:T(4,128)(2,1)}, u32[]{:S(2)}) copy-start(bf16[4,16384]{1,0:T(4,128)(2,1)} %param.20) | copy-start | bytes 393220
  36.0 33.3 %copy-start.61 = (bf16[384,512]{1,0:T(8,128)(2,1)}, bf16[384,512]{1,0:T(8,128)(2,1)S(1)}, u32[]{:S(2)}) copy-start(bf16[384,512]{1,0:T(8,128)(2,1)S(1)} %convert.112) | copy-start | bytes 1179652
  36.1 79.8 %copy-start.6 = (f32[256,512]{1,0:T(8,128)}, f32[256,512]{1,0:T(8,128)S(1)}, u32[]{:S(2)}) copy-start(f32[256,512]{1,0:T(8,128)S(1)} %slice.158) | copy-start | bytes 1572868
  36.8 33.1 %copy-start.78 = (f32[1024]{0:T(1024)}, f32[1024]{0:T(1024)S(1)}, u32[]{:S(2)}) copy-start(f32[1024]{0:T(1024)S(1)} %broadcast_subtract_fusion) | copy-start | bytes 12292
  46.1 25.1 %copy-start.88 = (f32[1,512]{1,0:T(1,128)}, f32[1,512]{1,0:T(1,128)S(1)}, u32[]{:S(2)}) copy-start(f32[1,512]{1,0:T(1,128)S(1)} %get-tuple-element.95) | copy-start | bytes 6148
  46.1 73.1 %copy-start.103 = (f32[1,512]{1,0:T(1,128)}, f32[1,512]{1,0:T(1,128)S(1)}, u32[]{:S(2)}) copy-start(f32[1,512]{1,0:T(1,128)S(1)} %get-tuple-element.93) | copy-start | bytes 6148
  46.1 154.7 %copy-start.106 = (f32[1,512]{1,0:T(1,128)}, f32[1,512]{1,0:T(1,128)S(1)}, u32[]{:S(2)}) copy-start(f32[1,512]{1,0:T(1,128)S(1)} %get-tuple-element.89) | copy-start | bytes 6148
  56.2 13.7 %copy-start.25 = (f32[1024,64]{1,0:T(8,128)}, f32[1024,64]{1,0:T(8,128)S(1)}, u32[]{:S(2)}) copy-start(f32[1024,64]{1,0:T(8,128)S(1)} %reshape.298) | copy-start | bytes 786436
  69.9 46.0 %copy-start = (f32[1024,512]{1,0:T(8,128)}, f32[1024,512]{1,0:T(8,128)S(1)}, u32[]{:S(2)}) copy-start(f32[1024,512]{1,0:T(8,128)S(1)} %get-tuple-element.97) | copy-start | bytes 6291460
  105.1 6.4 copy-start.53
  116.9 26.6 %copy-start.86 = (f32[1024]{0:T(1024)}, f32[1024]{0:T(1024)S(1)}, u32[]{:S(2)}) copy-start(f32[1024]{0:T(1024)S(1)} %broadcast_multiply_fusion.4) | copy-start | bytes 12292
  119.2 24.3 %copy-start.96 = (f32[1024]{0:T(1024)}, f32[1024]{0:T(1024)S(1)}, u32[]{:S(2)}) copy-start(f32[1024]{0:T(1024)S(1)} %fusion.144) | copy-start | bytes 12292
  149.7 48.3 %copy-start.8 = (f32[1024,512]{1,0:T(8,128)}, f32[1024,512]{1,0:T(8,128)S(1)}, u32[]{:S(2)}) copy-start(f32[1024,512]{1,0:T(8,128)S(1)} %get-tuple-element.104) | copy-start | bytes 6291460
  149.7 7.3 copy-start.109
  149.7 7.3 copy-start.123
  151.0 140.1 %copy-start.99 = (f32[1024]{0:T(1024)}, f32[1024]{0:T(1024)S(1)}, u32[]{:S(2)}) copy-start(f32[1024]{0:T(1024)S(1)} %fusion.145) | copy-start | bytes 12292
  187.3 6.3 copy-start.55
  200.7 56.2 %copy-start.101 = (f32[1024]{0:T(1024)}, f32[1024]{0:T(1024)S(1)}, u32[]{:S(2)}) copy-start(f32[1024]{0:T(1024)S(1)} %fusion.146) | copy-start | bytes 12292
  200.8 31.4 %copy-start.12 = (f32[1024,512]{1,0:T(8,128)S(1)}, f32[1024,512]{1,0:T(8,128)}, u32[]{:S(2)}) copy-start(f32[1024,512]{1,0:T(8,128)} %copy-done.11) | copy-start | bytes 6291460
  245.3 12.5 %copy-start.27 = (f32[1024,512]{1,0:T(8,128)}, f32[1024,512]{1,0:T(8,128)S(1)}, u32[]{:S(2)}) copy-start(f32[1024,512]{1,0:T(8,128)S(1)} %get-tuple-element.67) | copy-start | bytes 6291460
  246.1 7.4 copy-start.107
  246.1 7.4 copy-start.133
  267.5 10.3 %slice-start.2 = ((s8[8388608]{0:T(1024)(128)(4,1)}), s8[4194304]{0:T(1024)(128)(4,1)S(1)}, s32[]{:S(2)}) async-start(s8[8388608]{0:T(1024)(128)(4,1)} %bitcast.221), calls=%async_computation.29 | async-start | bytes 8388608
  292.1 15.3 %copy-start.33 = (f32[1024,512]{1,0:T(8,128)}, f32[1024,512]{1,0:T(8,128)S(1)}, u32[]{:S(2)}) copy-start(f32[1024,512]{1,0:T(8,128)S(1)} %add_add_fusion.7) | copy-start | bytes 6291460
  294.2 8.8 %copy-start.15 = (f32[1024,512]{1,0:T(8,128)S(1)}, f32[1024,512]{1,0:T(8,128)}, u32[]{:S(2)}) copy-start(f32[1024,512]{1,0:T(8,128)} %copy-done.14) | copy-start | bytes 6291460
  294.2 8.8 %copy-start.87 = (f32[1024]{0:T(1024)S(1)}, f32[1024]{0:T(1024)}, u32[]{:S(2)}) copy-start(f32[1024]{0:T(1024)} %copy-done.86) | copy-start | bytes 12292
  294.2 8.8 %copy-start.97 = (f32[1024]{0:T(1024)S(1)}, f32[1024]{0:T(1024)}, u32[]{:S(2)}) copy-start(f32[1024]{0:T(1024)} %copy-done.96) | copy-start | bytes 12292
  294.2 8.8 %copy-start.104 = (f32[1,512]{1,0:T(1,128)S(1)}, f32[1,512]{1,0:T(1,128)}, u32[]{:S(2)}) copy-start(f32[1,512]{1,0:T(1,128)} %copy-done.103) | copy-start | bytes 6148
  294.2 8.8 %copy-start.131 = (bf16[1,512,2048]{2,1,0:T(8,128)(2,1)S(1)}, bf16[1,512,2048]{2,1,0:T(8,128)(2,1)}, u32[]{:S(2)}) copy-start(bf16[1,512,2048]{2,1,0:T(8,128)(2,1)} %all-gather.17.cloned.1.call-done) | copy-start | bytes 6291460
  314.2 10.0 %slice-start = ((s8[8388608]{0:T(1024)(128)(4,1)}), s8[4194304]{0:T(1024)(128)(4,1)S(1)}, s32[]{:S(2)}) async-start(s8[8388608]{0:T(1024)(128)(4,1)} %bitcast.219), calls=%async_computation.27 | async-start | bytes 8388608
  347.1 52.8 %reduce-scatter.21.cloned.1.call-start = ((), (), s32[]{:S(2)}) async-start(), calls=%async_computation.13 | async-start | bytes 655360 | tf_op jit(solution)/shard_map/reduce_scatter | solution.py:203
  348.7 79.6 %reduce-scatter.19.cloned.1.call-start = ((), (), s32[]{:S(2)}) async-start(), calls=%async_computation.12 | async-start | bytes 655360 | tf_op jit(solution)/shard_map/reduce_scatter | solution.py:203
  352.4 110.4 %reduce-scatter.17.cloned.1.call-start = ((), (), s32[]{:S(2)}) async-start(), calls=%async_computation.11 | async-start | bytes 1966080 | tf_op jit(solution)/shard_map/reduce_scatter | solution.py:200
  358.0 139.2 %reduce-scatter.15.cloned.1.call-start = ((), (), s32[]{:S(2)}) async-start(), calls=%async_computation.10 | async-start | bytes 1966080 | tf_op jit(solution)/shard_map/reduce_scatter | solution.py:200
  363.1 172.7 %reduce-scatter.25.cloned.1.call-start = ((), (), s32[]{:S(2)}) async-start(), calls=%async_computation.15 | async-start | bytes 2621440 | tf_op jit(solution)/shard_map/reduce_scatter | solution.py:206
  363.2 6.2 copy-start.98
  363.2 6.2 copy-start.120
  369.3 205.5 %reduce-scatter.23.cloned.1.call-start = ((), (), s32[]{:S(2)}) async-start(), calls=%async_computation.14 | async-start | bytes 2621440 | tf_op jit(solution)/shard_map/reduce_scatter | solution.py:206
  377.0 236.5 %reduce-scatter.29.cloned.1.call-start = ((), (), s32[]{:S(2)}) async-start(), calls=%async_computation.17 | async-start | bytes 2621440 | tf_op jit(solution)/shard_map/reduce_scatter | solution.py:209
  384.6 267.8 %reduce-scatter.27.cloned.1.call-start = ((), (), s32[]{:S(2)}) async-start(), calls=%async_computation.16 | async-start | bytes 2621440 | tf_op jit(solution)/shard_map/reduce_scatter | solution.py:209
  392.2 303.3 %reduce-scatter.33.cloned.1.call-start = ((), (), s32[]{:S(2)}) async-start(), calls=%async_computation.25 | async-start | bytes 163840
  393.8 370.4 %all-reduce.3.cloned.1.call-start = ((), (), s32[]{:S(2)}) async-start(), calls=%async_computation.26 | async-start | bytes 6488064 | tf_op jit(solution)/shard_map/psum | solution.py:229
  654.7 133.4 %copy-start.92 = (f32[10,128]{1,0:T(8,128)S(1)}, f32[10,128]{1,0:T(8,128)}, u32[]{:S(2)}) copy-start(f32[10,128]{1,0:T(8,128)} %param.27) | copy-start | bytes 15364
  654.7 133.4 %copy-start.113 = (f32[10,128]{1,0:T(8,128)S(1)}, f32[10,128]{1,0:T(8,128)}, u32[]{:S(2)}) copy-start(f32[10,128]{1,0:T(8,128)} %param.33) | copy-start | bytes 15364
  654.7 133.4 %copy-start.114 = (f32[10,128]{1,0:T(8,128)S(1)}, f32[10,128]{1,0:T(8,128)}, u32[]{:S(2)}) copy-start(f32[10,128]{1,0:T(8,128)} %param.39) | copy-start | bytes 15364
  654.7 134.1 %copy-start.63 = (f32[384,128]{1,0:T(8,128)S(1)}, f32[384,128]{1,0:T(8,128)}, u32[]{:S(2)}) copy-start(f32[384,128]{1,0:T(8,128)} %param.26) | copy-start | bytes 589828
  654.7 134.0 %copy-start.67 = (f32[384,128]{1,0:T(8,128)S(1)}, f32[384,128]{1,0:T(8,128)}, u32[]{:S(2)}) copy-start(f32[384,128]{1,0:T(8,128)} %param.32) | copy-start | bytes 589828
  654.7 134.0 %copy-start.68 = (f32[384,128]{1,0:T(8,128)S(1)}, f32[384,128]{1,0:T(8,128)}, u32[]{:S(2)}) copy-start(f32[384,128]{1,0:T(8,128)} %param.38) | copy-start | bytes 589828
  764.2 6.5 copy-start.59
  764.2 7.2 copy-start.43
  764.2 24.6 %copy-start.66 = (bf16[384,128]{1,0:T(8,128)(2,1)S(1)}, bf16[384,128]{1,0:T(8,128)(2,1)}, u32[]{:S(2)}) copy-start(bf16[384,128]{1,0:T(8,128)(2,1)} %get-tuple-element.39) | copy-start | bytes 294916
  765.9 23.8 %copy-start.45 = (f32[2,128,512]{2,1,0:T(8,128)S(1)}, f32[2,128,512]{2,1,0:T(8,128)}, u32[]{:S(2)}) copy-start(f32[2,128,512]{2,1,0:T(8,128)} %param.23) | copy-start | bytes 1572868
  765.9 23.8 %copy-start.64 = (f32[2,128,512]{2,1,0:T(8,128)S(1)}, f32[2,128,512]{2,1,0:T(8,128)}, u32[]{:S(2)}) copy-start(f32[2,128,512]{2,1,0:T(8,128)} %param.29) | copy-start | bytes 1572868
  765.9 23.8 %copy-start.65 = (f32[2,128,512]{2,1,0:T(8,128)S(1)}, f32[2,128,512]{2,1,0:T(8,128)}, u32[]{:S(2)}) copy-start(f32[2,128,512]{2,1,0:T(8,128)} %param.35) | copy-start | bytes 1572868
  (96 other events, 240.9 us)
Sparse Core Ops, SparseCore 0:
  10.4 36.1 all-gather.14
  49.0 36.8 all-gather.16
  88.4 35.3 all-gather.18
  126.0 30.9 all-gather.20
  159.3 35.2 all-gather.22
  196.9 35.3 all-gather.24
  347.2 24.4 reduce-scatter.30
  375.1 24.7 reduce-scatter.20
  403.5 24.7 reduce-scatter.18
  431.7 30.9 reduce-scatter.16
  466.3 30.9 reduce-scatter.14
  500.6 35.1 reduce-scatter.24
  539.7 35.1 reduce-scatter.22
  578.3 35.1 reduce-scatter.28
  617.2 35.1 reduce-scatter.26
  655.6 23.8 reduce-scatter.32
  683.4 80.7 all-reduce.2
where the time goes:
time: 821 us; the launch traced here: 815 us
  waiting for transfers between devices  316 us (38%)
  matrix products  182 us (22%)
  blocking collectives  118 us (14%)
  local copies, waits for them, and re-layouts  109 us (13%)
  other arithmetic  64.7 us (8%)
  between operations  23.8 us (3%)
    reduce_scatter x2, waiting for transfers between devices, on_device(): lax.psum_scatter(grads[2].astype(jnp.bfloat16), 'shard', scatter_dimensio...  75.6 us
    dot_general x10, matrix products, dense(): return jnp.dot(left, right, preferred_element_type=jnp.float32)  75.3 us
    reduce_scatter x2, waiting for transfers between devices, on_device(): lax.psum_scatter(grads[3].astype(jnp.bfloat16), 'shard', scatter_dimensio...  75.2 us
    reduce_scatter x2, waiting for transfers between devices, on_device(): lax.psum_scatter(grads[0].astype(jnp.bfloat16), 'shard', scatter_dimensio...  67.2 us
    unnamed x301, local copies, waits for them, and re-layouts  56.2 us
    psum x1, waiting for transfers between devices, on_device(): lax.psum(as_sent(stacked + small), 'replica')  50.8 us
    dot_general x10, matrix products, dense_tn(): lax.dot_general(left, right, (((0,), (0,)), ((), ())), preferred_element_...  41.5 us
    psum x1, blocking collectives, on_device(): loss = lax.psum(local_error, ('shard', 'replica')) / count  39.5 us
  transfers between devices with their start and end apart: 17, of which 11 were waited for; matrix products, arithmetic and copies ran while one was open for 24% of the time, Pallas kernels for 0%

commit v1 on v0

v1 whole, which is shorter than its diff:
```python
import jax
import jax.numpy as jnp
from jax import lax
from jax.experimental import pallas as pl
from jax.experimental.pallas import tpu as pltpu
from jax.sharding import PartitionSpec as P

D = 512
H = 8
DH = 64
FF = 2048
P_SIZE = 64
LEN = 256
L = 2
MASKED = 102

EPS = 1e-05
CLIP = 0.001
RATE = 0.05
TABLE_RATE = 0.3
BETA_ONE = 0.9
BETA_TWO = 0.999
ADAM_EPS = 1e-08
DECAY = 0.1
STEP_COUNT = 10

W = 512
F32 = jnp.float32
BF16 = jnp.bfloat16


def dense(left, right):
    return jnp.dot(left, right, preferred_element_type=F32)


def dense_tn(left, right):
    return lax.dot_general(left, right, (((0,), (0,)), ((), ())), preferred_element_type=F32)


def dense_nt(left, right):
    return lax.dot_general(left, right, (((1,), (1,)), ((), ())), preferred_element_type=F32)


def layer_norm(x, gain, bias):
    center = x - jnp.mean(x, -1, keepdims=True)
    spread = jnp.mean(center * center, -1, keepdims=True)
    return center * lax.rsqrt(spread + EPS) * gain + bias


def params(**more):
    return pltpu.CompilerParams(vmem_limit_bytes=60 * 2**20, **more)


def cost(flops, data, trans=0):
    return pl.CostEstimate(flops=int(flops), bytes_accessed=int(data), transcendentals=int(trans))


def whole(shape):
    return pl.BlockSpec(shape, lambda *_: (0,) * len(shape))


ANY = pl.BlockSpec(memory_space=pl.ANY)
SMEM = pl.BlockSpec(memory_space=pltpu.SMEM)


def permute(x, axis, mask, size):
    return lax.ppermute(x, axis, [(i, i ^ mask) for i in range(size)])


def pick(x, index):
    return lax.dynamic_index_in_dim(x, index, 0, keepdims=False)


class Place:
    def __init__(self):
        self.shards = lax.axis_size("shard")
        self.replicas = lax.axis_size("replica")
        self.chips = self.replicas // 2
        self.shard = lax.axis_index("shard")
        replica = lax.axis_index("replica")
        self.core = replica % 2
        self.chip = replica // 2

    def to_core(self, x):
        return permute(x, "replica", 1, self.replicas)

    def to_shard(self, x, mask):
        return permute(x, "shard", mask, self.shards)

    def to_chip(self, x, mask):
        return permute(x, "replica", 2 * mask, self.replicas)


def gather_group(place, mine):
    ours = [place.to_shard(mine, mask) for mask in range(1, place.shards)]
    return ours, [place.to_core(part) for part in ours]


def stages_of(size):
    found = []
    bit = 1
    while bit < size:
        radix = 4 if bit * 4 <= size else 2
        found.append((bit, radix))
        bit *= radix
    return found


def add_up(parts):
    total = parts[0].astype(F32)
    for part in parts[1:]:
        total = total + part.astype(F32)
    return total.astype(BF16)


def reduce_chips(place, x):
    stages = stages_of(place.chips)
    for bit, radix in stages:
        digit = (place.chip // bit) % radix
        x = x.reshape((radix, x.shape[0] // radix) + x.shape[1:])
        got = [place.to_chip(pick(x, digit ^ k), k * bit) for k in range(1, radix)]
        x = add_up([pick(x, digit)] + got)
    for bit, radix in reversed(stages):
        digit = (place.chip // bit) % radix
        got = [x] + [place.to_chip(x, k * bit) for k in range(1, radix)]
        x = jnp.concatenate([select_of(got, digit ^ k) for k in range(radix)], 0)
    return x


def select_of(items, index):
    out = items[0]
    for k in range(1, len(items)):
        out = jnp.where(index == k, items[k], out)
    return out


def reduce_shards(place, keep, other):
    pieces = [
        add_up([pick(keep, place.shard ^ k), pick(other, place.shard ^ k)])
        for k in range(place.shards)
    ]
    return add_up([pieces[0]] + [place.to_shard(pieces[k], k) for k in range(1, place.shards)])


def fill_weights(step, where_ref, sources, targets, sem):
    shard, core = where_ref[0], where_ref[1]
    count = (len(sources) - 1) // 2

    def copies():
        made = []
        for piece, index in [(sources[0], None)] + [(s, k) for k, s in enumerate(sources[1:])]:
            if index is None:
                at, half = shard, None
            else:
                at = shard ^ (index % count + 1)
                half = core if index < count else 1 - core
            made += targets(piece, at, half)
        return [pltpu.make_async_copy(s, t, sem.at[n]) for n, (s, t) in enumerate(made)]

    @pl.when(step == 0)
    def _():
        todo = copies()
        for copy in todo:
            copy.start()
        for copy in todo:
            copy.wait()


def attn_targets(w_ref, rows):
    def targets(piece, at, half):
        at = pl.ds(pl.multiple_of(at * rows, rows), rows)
        if half is None:
            return [(piece.at[h], w_ref.at[pl.ds(2 * h, 2), at]) for h in range(2)]
        return [(piece, w_ref.at[pl.ds(half * 2, 2), at])]

    return targets


def mlp_targets(up_ref, down_ref, rows):
    def one(piece, at, half):
        spot = pl.ds(pl.multiple_of(at * rows, rows), rows)
        return [
            (piece.at[pl.ds(0, 2)], up_ref.at[pl.ds(half * 2, 2), spot]),
            (piece.at[pl.ds(2, 2)], down_ref.at[pl.ds(at * 4 + half * 2, 2)]),
        ]

    def targets(piece, at, half):
        if half is None:
            return one(piece.at[0], at, 0) + one(piece.at[1], at, 1)
        return one(piece, at, half)

    return targets


def norm_parts(x):
    center = x - jnp.mean(x, -1, keepdims=True)
    rstd = lax.rsqrt(jnp.mean(center * center, -1, keepdims=True) + EPS)
    return center * rstd, rstd


def norm_back(xhat, rstd, dy, gain):
    dxh = dy * gain
    return rstd * (
        dxh - jnp.mean(dxh, -1, keepdims=True) - xhat * jnp.mean(dxh * xhat, -1, keepdims=True)
    )


def attn_fwd(place, where, x, norms, group):
    rows = D // place.shards
    seqs = x.shape[0] // LEN
    sources = len(group)

    def kernel(where_ref, x_ref, norm_ref, *refs):
        pieces, refs = refs[:sources], refs[sources:]
        mid_ref, qkv_ref, pt_ref, ot_ref, w_ref, sem = refs
        fill_weights(pl.program_id(0), where_ref, pieces, attn_targets(w_ref, rows), sem)
        x = x_ref[...]
        xhat, _ = norm_parts(x)
        a = (xhat * norm_ref[0:1, :] + norm_ref[1:2, :]).astype(BF16)
        q = (dense(a, w_ref[0]) * DH**-0.5).astype(BF16)
        k = dense(a, w_ref[1]).astype(BF16)
        v = dense(a, w_ref[2]).astype(BF16)
        qkv_ref[:, :D] = q
        qkv_ref[:, D : 2 * D] = k
        qkv_ref[:, 2 * D :] = v
        vt = v.T
        lane = lax.broadcasted_iota(jnp.int32, (LEN, 128), 1)
        for h in range(H):
            pair = slice(128 * (h // 2), 128 * (h // 2) + 128)
            one = slice(DH * h, DH * h + DH)
            own = (lane < DH) if h % 2 == 0 else (lane >= DH)
            st = dense_nt(k[:, pair], jnp.where(own, q[:, pair], 0))
            e = jnp.exp(st - jnp.max(st, axis=0, keepdims=True))
            p = (e * (1.0 / jnp.sum(e, axis=0, keepdims=True))).astype(BF16)
            pt_ref[h] = p
            ot_ref[one, :] = dense(vt[one, :], p).astype(BF16)
        mid_ref[...] = x + dense_tn(ot_ref[...], w_ref[3])

    n = x.shape[0]
    return pl.pallas_call(
        kernel,
        grid=(seqs,),
        in_specs=[SMEM, pl.BlockSpec((LEN, D), lambda i: (i, 0)), whole((4, D))] + [ANY] * sources,
        out_specs=[
            pl.BlockSpec((LEN, D), lambda i: (i, 0)),
            pl.BlockSpec((LEN, 3 * D), lambda i: (i, 0)),
            pl.BlockSpec((None, H, LEN, LEN), lambda i: (i, 0, 0, 0)),
            pl.BlockSpec((None, D, LEN), lambda i: (i, 0, 0)),
        ],
        out_shape=[
            jax.ShapeDtypeStruct((n, D), F32),
            jax.ShapeDtypeStruct((n, 3 * D), BF16),
            jax.ShapeDtypeStruct((seqs, H, LEN, LEN), BF16),
            jax.ShapeDtypeStruct((seqs, D, LEN), BF16),
        ],
        scratch_shapes=[pltpu.VMEM((4, D, W), BF16), pltpu.SemaphoreType.DMA((2 * sources,))],
        compiler_params=params(),
        cost_estimate=cost(2 * n * D * (4 * D + 2 * LEN), n * D * 20, n * H * LEN),
        name="attn_fwd",
    )(where, x, norms, *group)


def gelu_pair(u):
    z = jnp.abs(u) * 0.7071067811865476
    t = 1.0 / (1.0 + 0.3275911 * z)
    poly = t * (
        0.254829592
        + t * (-0.284496736 + t * (1.421413741 + t * (-1.453152027 + t * 1.061405429)))
    )
    e = jnp.exp(-z * z)
    tail = 0.5 * poly * e
    cdf = jnp.where(u >= 0, 1.0 - tail, tail)
    return u * cdf, cdf + u * e * 0.3989422804014327


def mlp_fwd(place, where, mid, norms, group):
    rows = D // place.shards
    n = mid.shape[0]
    sources = len(group)
    per = W // rows

    def kernel(where_ref, mid_ref, norm_ref, *refs):
        pieces, refs = refs[:sources], refs[sources:]
        out_ref, act_ref, gp_ref, up_ref, down_ref, sem = refs
        fill_weights(pl.program_id(0), where_ref, pieces, mlp_targets(up_ref, down_ref, rows), sem)
        mid = mid_ref[...]
        xhat, _ = norm_parts(mid)
        c = (xhat * norm_ref[2:3, :] + norm_ref[3:4, :]).astype(BF16)
        total = mid
        for b in range(FF // W):
            cols = slice(W * b, W * b + W)
            act, slope = gelu_pair(dense(c, up_ref[b]))
            act = act.astype(BF16)
            act_ref[:, cols] = act
            gp_ref[:, cols] = slope.astype(BF16)
            total = total + dense(act, down_ref[per * b : per * b + per].reshape(W, D))
        out_ref[...] = total

    return pl.pallas_call(
        kernel,
        grid=(n // LEN,),
        in_specs=[SMEM, pl.BlockSpec((LEN, D), lambda i: (i, 0)), whole((4, D))] + [ANY] * sources,
        out_specs=[
            pl.BlockSpec((LEN, D), lambda i: (i, 0)),
            pl.BlockSpec((LEN, FF), lambda i: (i, 0)),
            pl.BlockSpec((LEN, FF), lambda i: (i, 0)),
        ],
        out_shape=[
            jax.ShapeDtypeStruct((n, D), F32),
            jax.ShapeDtypeStruct((n, FF), BF16),
            jax.ShapeDtypeStruct((n, FF), BF16),
        ],
        scratch_shapes=[
            pltpu.VMEM((4, D, W), BF16),
            pltpu.VMEM((FF // rows, rows, D), BF16),
            pltpu.SemaphoreType.DMA((2 * sources + 2,)),
        ],
        compiler_params=params(),
        cost_estimate=cost(4 * n * D * FF, n * D * 24, n * FF * 2),
        name="mlp_fwd",
    )(where, mid, norms, *group)


def mlp_bwd(place, where, dz, mid, act, gp, norms, group):
    rows = D // place.shards
    n = mid.shape[0]
    sources = len(group)
    per = W // rows

    def kernel(where_ref, dz_ref, mid_ref, gp_ref, norm_ref, *refs):
        pieces, refs = refs[:sources], refs[sources:]
        dmid_ref, du_ref, c_ref, dm_ref, dn_ref, up_ref, down_ref, sem = refs
        i = pl.program_id(0)
        fill_weights(i, where_ref, pieces, mlp_targets(up_ref, down_ref, rows), sem)
        dz = dz_ref[...]
        dm = dz.astype(BF16)
        dm_ref[...] = dm
        xhat, rstd = norm_parts(mid_ref[...])
        gain = norm_ref[2:3, :]
        c_ref[...] = (xhat * gain + norm_ref[3:4, :]).astype(BF16)
        dc = jnp.zeros((LEN, D), F32)
        for b in range(FF // W):
            cols = slice(W * b, W * b + W)
            da = dense_nt(dm, down_ref[per * b : per * b + per].reshape(W, D))
            du = (gp_ref[:, cols].astype(F32) * da).astype(BF16)
            du_ref[:, cols] = du
            dc = dc + dense_nt(du, up_ref[b])
        dmid_ref[...] = dz + norm_back(xhat, rstd, dc, gain)

        @pl.when(i == 0)
        def _():
            dn_ref[...] = jnp.zeros_like(dn_ref)

        dn_ref[0:1, :] += jnp.sum(dc * xhat, 0, keepdims=True)
        dn_ref[1:2, :] += jnp.sum(dc, 0, keepdims=True)

    def row(width):
        return pl.BlockSpec((LEN, width), lambda i: (i, 0))

    return pl.pallas_call(
        kernel,
        grid=(n // LEN,),
        in_specs=[SMEM, row(D), row(D), row(FF), whole((4, D))] + [ANY] * sources,
        out_specs=[row(D), row(FF), row(D), row(D), whole((8, D))],
        out_shape=[
            jax.ShapeDtypeStruct((n, D), F32),
            jax.ShapeDtypeStruct((n, FF), BF16),
            jax.ShapeDtypeStruct((n, D), BF16),
            jax.ShapeDtypeStruct((n, D), BF16),
            jax.ShapeDtypeStruct((8, D), F32),
        ],
        scratch_shapes=[
            pltpu.VMEM((4, D, W), BF16),
            pltpu.VMEM((FF // rows, rows, D), BF16),
            pltpu.SemaphoreType.DMA((2 * sources + 2,)),
        ],
        compiler_params=params(),
        cost_estimate=cost(4 * n * D * FF, n * D * 32),
        name="mlp_bwd",
    )(where, dz, mid, gp, norms, *group)


def attn_bwd(place, where, dmid, x, qkv, pt, ot, norms, group):
    rows = D // place.shards
    n = x.shape[0]
    seqs = n // LEN
    sources = len(group)

    def kernel(where_ref, dmid_ref, x_ref, qkv_ref, pt_ref, ot_ref, norm_ref, *refs):
        pieces, refs = refs[:sources], refs[sources:]
        dx_ref, dqkv_ref, a_ref, dh_ref, dn_ref, w_ref, dqt_ref, sem = refs
        i = pl.program_id(0)
        fill_weights(i, where_ref, pieces, attn_targets(w_ref, rows), sem)
        dmid = dmid_ref[...]
        dh = dmid.astype(BF16)
        dh_ref[...] = dh
        do = dense_nt(dh, w_ref[3]).astype(BF16)
        along = do.T.astype(F32) * ot_ref[...].astype(F32)
        q = qkv_ref[:, :D]
        k = qkv_ref[:, D : 2 * D]
        v = qkv_ref[:, 2 * D :]
        kt = k.T
        lane = lax.broadcasted_iota(jnp.int32, (LEN, 128), 1)
        for j in range(H // 2):
            pair = slice(128 * j, 128 * j + 128)
            dk = jnp.zeros((LEN, 128), F32)
            dv = jnp.zeros((LEN, 128), F32)
            for h in (2 * j, 2 * j + 1):
                one = slice(DH * h, DH * h + DH)
                own = (lane < DH) if h % 2 == 0 else (lane >= DH)
                doh = jnp.where(own, do[:, pair], 0)
                pth = pt_ref[h]
                dpt = dense_nt(v[:, pair], doh)
                delta = jnp.sum(along[one, :], axis=0, keepdims=True)
                dst = (pth.astype(F32) * (dpt - delta)).astype(BF16)
                dv = dv + dense(pth, doh)
                dk = dk + dense(dst, jnp.where(own, q[:, pair], 0))
                dqt_ref[one, :] = (dense(kt[one, :], dst) * DH**-0.5).astype(BF16)
            dqkv_ref[:, D + 128 * j : D + 128 * j + 128] = dk.astype(BF16)
            dqkv_ref[:, 2 * D + 128 * j : 2 * D + 128 * j + 128] = dv.astype(BF16)
        dqkv_ref[:, :D] = dqt_ref[...].T
        da = dense_nt(dqkv_ref[:, :D], w_ref[0])
        da = da + dense_nt(dqkv_ref[:, D : 2 * D], w_ref[1])
        da = da + dense_nt(dqkv_ref[:, 2 * D :], w_ref[2])
        xhat, rstd = norm_parts(x_ref[...])
        gain = norm_ref[0:1, :]
        a_ref[...] = (xhat * gain + norm_ref[1:2, :]).astype(BF16)
        dx_ref[...] = dmid + norm_back(xhat, rstd, da, gain)

        @pl.when(i == 0)
        def _():
            dn_ref[...] = jnp.zeros_like(dn_ref)

        dn_ref[0:1, :] += jnp.sum(da * xhat, 0, keepdims=True)
        dn_ref[1:2, :] += jnp.sum(da, 0, keepdims=True)

    def row(width):
        return pl.BlockSpec((LEN, width), lambda i: (i, 0))

    return pl.pallas_call(
        kernel,
        grid=(seqs,),
        in_specs=[
            SMEM,
            row(D),
            row(D),
            row(3 * D),
            pl.BlockSpec((None, H, LEN, LEN), lambda i: (i, 0, 0, 0)),
            pl.BlockSpec((None, D, LEN), lambda i: (i, 0, 0)),
            whole((4, D)),
        ]
        + [ANY] * sources,
        out_specs=[row(D), row(3 * D), row(D), row(D), whole((8, D))],
        out_shape=[
            jax.ShapeDtypeStruct((n, D), F32),
            jax.ShapeDtypeStruct((n, 3 * D), BF16),
            jax.ShapeDtypeStruct((n, D), BF16),
            jax.ShapeDtypeStruct((n, D), BF16),
            jax.ShapeDtypeStruct((8, D), F32),
        ],
        scratch_shapes=[
            pltpu.VMEM((4, D, W), BF16),
            pltpu.VMEM((D, LEN), BF16),
            pltpu.SemaphoreType.DMA((2 * sources,)),
        ],
        compiler_params=params(),
        cost_estimate=cost(2 * n * D * (4 * D + 5 * LEN), n * D * 32),
        name="attn_bwd",
    )(where, dmid, x, qkv, pt, ot, norms, *group)


def grad_mlp(place, where, c, du, act, dm):
    shards = place.shards
    rows = D // shards
    n = c.shape[0]
    wide = FF // (2 * shards)

    def half_of(p, where_ref):
        return where_ref[1] ^ (1 - p)

    def kernel(where_ref, c_ref, du_ref, act_ref, dm_ref, send_ref, keep_ref, ct_ref):
        p, i = pl.program_id(0), pl.program_id(1)

        @pl.when((p == 0) & (i == 0))
        def _():
            ct_ref[...] = c_ref[...].T

        def put(out_ref):
            @pl.when(i < 2)
            def _():
                out_ref[:, i] = dense(ct_ref[...], du_ref[...]).astype(BF16).reshape(shards, rows, W)

            @pl.when(i >= 2)
            def _():
                block = dense_tn(act_ref[...], dm_ref[...]).astype(BF16)
                out_ref[i - 2, 2:4] = block.reshape(2, rows, W)

        @pl.when(p == 0)
        def _():
            put(send_ref)

        @pl.when(p == 1)
        def _():
            put(keep_ref)

    shape = (shards, 4, rows, W)
    return pl.pallas_call(
        kernel,
        grid_spec=pltpu.PrefetchScalarGridSpec(
            num_scalar_prefetch=1,
            grid=(2, 2 + shards),
            in_specs=[
                whole((n, D)),
                pl.BlockSpec((n, W), lambda p, i, w: (0, 2 * half_of(p, w) + jnp.minimum(i, 1))),
                pl.BlockSpec(
                    (n, wide), lambda p, i, w: (0, 2 * jnp.maximum(i - 2, 0) + half_of(p, w))
                ),
                whole((n, D)),
            ],
            out_specs=[whole(shape), whole(shape)],
            scratch_shapes=[pltpu.VMEM((D, n), BF16)],
        ),
        out_shape=[jax.ShapeDtypeStruct(shape, BF16)] * 2,
        compiler_params=params(),
        cost_estimate=cost(4 * n * D * FF, n * (4 * D + 4 * FF) + 4 * D * FF),
        name="grad_mlp",
    )(where, c, du, act, dm)


def grad_attn(place, where, a, dqkv, ot, dh):
    shards = place.shards
    rows = D // shards
    n = a.shape[0]
    seqs = n // LEN

    def block_of(p, i, where_ref):
        return 2 * (where_ref[1] ^ (1 - p)) + i

    def kernel(where_ref, a_ref, dqkv_ref, ot_ref, dh_ref, send_ref, keep_ref, at_ref):
        p, i = pl.program_id(0), pl.program_id(1)
        block = block_of(p, i, where_ref)

        @pl.when((p == 0) & (i == 0))
        def _():
            at_ref[...] = a_ref[...].T

        def put(out_ref):
            @pl.when(block < 3)
            def _():
                out_ref[:, i] = dense(at_ref[...], dqkv_ref[...]).astype(BF16).reshape(shards, rows, W)

            @pl.when(block == 3)
            def _():
                total = dense(ot_ref[0], dh_ref[:LEN, :])
                for s in range(1, seqs):
                    total = total + dense(ot_ref[s], dh_ref[LEN * s : LEN * s + LEN, :])
                out_ref[:, i] = total.astype(BF16).reshape(shards, rows, W)

        @pl.when(p == 0)
        def _():
            put(send_ref)

        @pl.when(p == 1)
        def _():
            put(keep_ref)

    shape = (shards, 2, rows, W)
    return pl.pallas_call(
        kernel,
        grid_spec=pltpu.PrefetchScalarGridSpec(
            num_scalar_prefetch=1,
            grid=(2, 2),
            in_specs=[
                whole((n, D)),
                pl.BlockSpec((n, W), lambda p, i, w: (0, jnp.minimum(block_of(p, i, w), 2))),
                whole((seqs, D, LEN)),
                whole((n, D)),
            ],
            out_specs=[whole(shape), whole(shape)],
            scratch_shapes=[pltpu.VMEM((D, n), BF16)],
        ),
        out_shape=[jax.ShapeDtypeStruct(shape, BF16)] * 2,
        compiler_params=params(),
        cost_estimate=cost(8 * n * D * D, n * 14 * D + 8 * D * D),
        name="grad_attn",
    )(where, a, dqkv, ot, dh)


def adam(weight, first, second, grad, rate):
    first = BETA_ONE * first + (1 - BETA_ONE) * grad
    second = BETA_TWO * second + (1 - BETA_TWO) * grad * grad
    fixed_one = first / (1 - BETA_ONE**STEP_COUNT)
    fixed_two = second / (1 - BETA_TWO**STEP_COUNT)
    weight = weight - rate * (fixed_one / (jnp.sqrt(fixed_two) + ADAM_EPS) + DECAY * weight)
    return (weight, first, second)


def on_device(
    series,
    mask,
    qkv_w,
    out_w,
    up_w,
    down_w,
    patch_maps,
    norm_params,
    qkv_m,
    out_m,
    up_m,
    down_m,
    patch_m,
    norm_m,
    qkv_v,
    out_v,
    up_v,
    down_v,
    patch_v,
    norm_v,
):
    place = Place()
    shards = place.shards
    rows = D // shards
    seqs = series.shape[0]
    count = MASKED * seqs * shards * place.replicas
    where = jnp.stack([place.shard, place.core]).astype(jnp.int32)

    small_rows = 400
    table = jnp.concatenate(
        [patch_maps, norm_params, jnp.zeros((small_rows - 394, rows), F32)], 0
    ).reshape(2, small_rows // 2, rows)
    ours, theirs = gather_group(place, pick(table, place.core))
    parts = [table] + [
        jnp.where(place.core == 0, jnp.stack([a, b]), jnp.stack([b, a])) for a, b in zip(ours, theirs)
    ]
    maps = jnp.concatenate(
        [select_of(parts, place.shard ^ j).reshape(small_rows, rows) for j in range(shards)], 1
    )
    embed = maps[:P_SIZE].astype(BF16)
    head = maps[P_SIZE : 2 * P_SIZE].astype(BF16)
    pos = maps[2 * P_SIZE : 2 * P_SIZE + LEN]
    norms_all = maps[2 * P_SIZE + LEN : 2 * P_SIZE + LEN + 4 * L + 2]

    attn_groups = []
    mlp_groups = []
    for index in range(L):
        cols = qkv_w[index].reshape(rows, 3, W)
        local = jnp.concatenate([cols.transpose(1, 0, 2), out_w[index][None]], 0).astype(BF16)
        local = local.reshape(2, 2, rows, W)
        ours, theirs = gather_group(place, pick(local, place.core))
        attn_groups.append([local] + ours + theirs)
        up = up_w[index].reshape(rows, 2, 2, W).transpose(1, 2, 0, 3)
        down = down_w[index].reshape(2, 2, rows, W)
        local = jnp.concatenate([up, down], 1).astype(BF16)
        ours, theirs = gather_group(place, pick(local, place.core))
        mlp_groups.append([local] + ours + theirs)

    target = series.reshape(seqs * LEN, P_SIZE).astype(F32)
    maskf = mask.reshape(seqs * LEN, 1).astype(F32)
    inputs = (target * (1.0 - maskf)).astype(BF16)
    x = dense(inputs, embed) + jnp.tile(pos, (seqs, 1))
    saved = []
    for index in range(L):
        norms = norms_all[4 * index : 4 * index + 4]
        mid, qkv, pt, ot = attn_fwd(place, where, x, norms, attn_groups[index])
        y, act, gp = mlp_fwd(place, where, mid, norms, mlp_groups[index])
        saved.append((x, mid, qkv, pt, ot, act, gp, norms))
        x = y

    final = layer_norm(x, norms_all[4 * L], norms_all[4 * L + 1])
    final_low = final.astype(BF16)
    err = dense_nt(final_low, head) - target
    loss = jnp.sum(maskf * jnp.mean(err * err, -1, keepdims=True)).reshape(1, 1)
    grad_pred = (maskf * err * (2.0 / (P_SIZE * count))).astype(BF16)
    g_head = dense_tn(grad_pred, final_low)
    _, final_back = jax.vjp(layer_norm, x, norms_all[4 * L], norms_all[4 * L + 1])
    grad, gain_f, bias_f = final_back(dense(grad_pred, head))

    pieces = []
    norm_grads = [None] * L
    for index in reversed(range(L)):
        x, mid, qkv, pt, ot, act, gp, norms = saved[index]
        dmid, du, c, dm, dn_mlp = mlp_bwd(place, where, grad, mid, act, gp, norms, mlp_groups[index])
        send, keep = grad_mlp(place, where, c, du, act, dm)
        piece_mlp = reduce_shards(place, keep, place.to_core(send))
        grad, dqkv, a, dh, dn_attn = attn_bwd(
            place, where, dmid, x, qkv, pt, ot, norms, attn_groups[index]
        )
        send, keep = grad_attn(place, where, a, dqkv, ot, dh)
        piece_attn = reduce_shards(place, keep, place.to_core(send))
        norm_grads[index] = jnp.concatenate([dn_attn[:2], dn_mlp[:2]], 0)
        piece_mlp = reduce_chips(place, piece_mlp.reshape(4 * rows, W))
        piece_attn = reduce_chips(place, piece_attn.reshape(2 * rows, W))
        pieces.append((index, piece_attn, piece_mlp))

    g_embed = dense_tn(inputs, grad.astype(BF16))
    g_table = jnp.sum(grad.reshape(seqs, LEN, D), 0)
    g_small = jnp.concatenate(
        [g_embed, g_head, g_table] + norm_grads + [jnp.stack([gain_f, bias_f])], 0
    )
    g_small = jnp.pad(g_small, ((0, small_rows - g_small.shape[0]), (0, 0))).astype(BF16)
    g_small = g_small.reshape(2, small_rows // 2, shards, rows).transpose(0, 2, 1, 3)
    other = place.to_core(pick(g_small, 1 - place.core))
    piece = reduce_shards(place, pick(g_small, place.core), other)
    pad = -piece.shape[0] % (8 * place.chips)
    piece = reduce_chips(place, jnp.pad(piece, ((0, pad), (0, 0))))
    piece_small = piece[: small_rows // 2]

    for bit in range(shards.bit_length() - 1):
        loss = loss + place.to_shard(loss, 1 << bit)
    for bit in range(place.chips.bit_length() - 1):
        loss = loss + place.to_chip(loss, 1 << bit)
    loss = (loss + place.to_core(loss)).reshape(()) / count

    squares = jnp.zeros((), F32)
    for part in [piece_small] + [p for _, a, b in pieces for p in (a, b)]:
        part = part.astype(F32)
        squares = squares + jnp.sum(part * part)
    squares = squares.reshape(1, 1)
    squares = squares + place.to_core(squares)
    squares = sum([place.to_shard(squares, k) for k in range(1, shards)], squares)
    grad_norm = jnp.sqrt(squares.reshape(()))
    factor = CLIP / jnp.maximum(grad_norm, CLIP)

    def halves(mine):
        other = place.to_core(mine)
        first = jnp.where(place.core == 0, mine, other)
        second = jnp.where(place.core == 0, other, mine)
        return first, second

    big = [None] * L
    for index, piece_attn, piece_mlp in pieces:
        low, high = halves(piece_attn)
        low, high = low.reshape(2, rows, W), high.reshape(2, rows, W)
        g_qkv = jnp.concatenate([low[0], low[1], high[0]], 1)
        g_out = high[1]
        low, high = halves(piece_mlp)
        low, high = low.reshape(4, rows, W), high.reshape(4, rows, W)
        g_up = jnp.concatenate([low[0], low[1], high[0], high[1]], 1)
        g_down = jnp.concatenate([low[2:].reshape(2 * rows, W), high[2:].reshape(2 * rows, W)], 0)
        big[index] = (g_qkv, g_out, g_up, g_down)
    low, high = halves(piece_small)
    g_small = jnp.concatenate([low, high], 0)
    grads_all = tuple(jnp.stack([big[i][j] for i in range(L)]) for j in range(4))
    grads_all = grads_all + (g_small[:384], g_small[384:394])

    weights = (qkv_w, out_w, up_w, down_w, patch_maps, norm_params)
    firsts = (qkv_m, out_m, up_m, down_m, patch_m, norm_m)
    seconds = (qkv_v, out_v, up_v, down_v, patch_v, norm_v)
    rates = (RATE, RATE, RATE, RATE, TABLE_RATE, TABLE_RATE)
    results = [
        adam(w, m, v, g.astype(F32) * factor, r)
        for w, m, v, g, r in zip(weights, firsts, seconds, grads_all, rates)
    ]
    news = tuple(r[0] for r in results)
    new_m = tuple(r[1] for r in results)
    new_v = tuple(r[2] for r in results)
    return (loss, grad_norm) + news + new_m + new_v


def solution(mesh):
    batch = P(("shard", "replica"), None)
    stack = P(None, "shard", None)
    flat = P(None, "shard")
    state = (stack, stack, stack, stack, flat, flat)
    return jax.shard_map(
        on_device,
        mesh=mesh,
        in_specs=(batch, batch) + state * 3,
        out_specs=(P(), P()) + state * 3,
        check_vma=False,
    )
```

time: 821 us -> 532 us (0.65)
  Pallas kernels: 0 us -> 192 us
  waiting for transfers between devices: 316 us -> 126 us
  matrix products: 182 us -> 8.55 us
  blocking collectives: 118 us -> 0 us
  starting transfers between devices: 1.16 us -> 106 us
  local copies, waits for them, and re-layouts: 109 us -> 20 us
  other arithmetic: 64.7 us -> 54.2 us
  between operations: 23.8 us -> 14.6 us
    reduce_scatter x8 -> x0, waiting for transfers between devices: 251 us -> none  [the longest x2 75.6 us: on_device(): lax.psum_scatter(grads[2].astype(jnp.bfloat16), 'shard', scatter_dimensio...]
    pallas_call x0 -> x12, Pallas kernels: none -> 192 us  [the longest x2 45.9 us: attn_bwd(): pl.pallas_call(kernel, grid=(seqs,), in_specs=[SMEM, row(D), row(D), row(...]
    ppermute x0 -> x94, waiting for transfers between devices: none -> 126 us  [permute(): return lax.ppermute(x, axis, [(i, i ^ mask) for i in range(size)])]
    ppermute x0 -> x94, starting transfers between devices: none -> 106 us  [permute(): return lax.ppermute(x, axis, [(i, i ^ mask) for i in range(size)])]
    dot_general x22 -> x2, matrix products: 107 us -> 4.7 us  [dense(): return jnp.dot(left, right, preferred_element_type=F32)]
    psum x3 -> x0, blocking collectives: 66.4 us -> none  [the longest x1 39.5 us: on_device(): loss = lax.psum(local_error, ('shard', 'replica')) / count]
    all_gather x4 -> x0, blocking collectives: 51.5 us -> none  [the longest x2 21.9 us: gather_layer(): lax.all_gather(pieces[1], 'shard', axis=0, tiled=True)]
    psum x1 -> x0, waiting for transfers between devices: 50.8 us -> none  [on_device(): lax.psum(as_sent(stacked + small), 'replica')]
  transfers between devices with their start and end apart: 17 -> 94, of which waited for: 11 -> 33; matrix products, arithmetic and copies ran while one was open for 24% -> 11% of each run, Pallas kernels for 0% -> 33%
where the time goes in v1:
time: 532 us; the launch traced here: 521 us
  Pallas kernels  192 us (36%)
  waiting for transfers between devices  126 us (24%)
  starting transfers between devices  106 us (20%)
  other arithmetic  54.2 us (10%)
  local copies, waits for them, and re-layouts  20 us (4%)
  between operations  14.6 us (3%)
  matrix products  8.55 us (2%)
    ppermute x94, waiting for transfers between devices, permute(): return lax.ppermute(x, axis, [(i, i ^ mask) for i in range(size)])  126 us
    ppermute x94, starting transfers between devices, permute(): return lax.ppermute(x, axis, [(i, i ^ mask) for i in range(size)])  106 us
    pallas_call x2, Pallas kernels, attn_bwd(): pl.pallas_call(kernel, grid=(seqs,), in_specs=[SMEM, row(D), row(D), row(...  45.9 us
    pallas_call x2, Pallas kernels, attn_fwd(): pl.pallas_call(kernel, grid=(seqs,), in_specs=[SMEM, pl.BlockSpec((LEN, D...  37.2 us
    pallas_call x2, Pallas kernels, mlp_fwd(): pl.pallas_call(kernel, grid=(n // LEN,), in_specs=[SMEM, pl.BlockSpec((LE...  36.5 us
    pallas_call x2, Pallas kernels, grad_mlp(): pl.pallas_call(kernel, grid_spec=pltpu.PrefetchScalarGridSpec(num_scalar_...  30 us
    pallas_call x2, Pallas kernels, mlp_bwd(): pl.pallas_call(kernel, grid=(n // LEN,), in_specs=[SMEM, row(D), row(D),...  25.8 us
    sub x6, other arithmetic, adam(): weight - rate * (fixed_one / (jnp.sqrt(fixed_two) + ADAM_EPS) + DECAY * w...  17.2 us
  transfers between devices with their start and end apart: 94, of which 33 were waited for; matrix products, arithmetic and copies ran while one was open for 11% of the time, Pallas kernels for 33%

profile of v1, /device:TPU:0, one launch (start us, length us, event | category | flops | bytes accessed | tf_op | source)
XLA Modules:
  0.0 521.2 jit_solution(6747667732505299362)
XLA Ops:
  2.6 2.9 collective-permute-start.4
  10.7 2.9 collective-permute-start.8
  25.3 2.9 collective-permute-start.20
  32.8 4.8 collective-permute-done.20.refs_3_
  38.6 3.2 collective-permute-done.19.refs_2_
  49.3 30.2 %collective-permute-done.26.refs_3_ = bf16[4,128,512]{2,1,0:T(8,128)(2,1)S(1)} collective-permute-done((bf16[4,128,512]{2,1,0:T(8,128)(2,1)}, bf16[4,128,512]{2,1,0:T(8,128)(2,1)S(1)}, u32[]{:S(2)}, u32[]{:S(2)}) %collective-permute-start.26) | collective-permute-done | bytes 524320 | tf_op jit(solution)/shard_map/ppermute | solution.py:67
  80.8 1.8 bitcast_add_fusion.x_ref
  83.2 18.5 %attn_fwd.2 = (f32[1024,512]{1,0:T(8,128)}, bf16[1024,1536]{1,0:T(8,128)(2,1)}, bf16[4,8,256,256]{3,2,1,0:T(8,128)(2,1)}, bf16[4,512,256]{2,1,0:T(8,128)(2,1)}) custom-call(s32[2]{0:T(128)} %pad_add_fusion.where_ref, f32[1024,512]{1,0:T(8,128)} %bitcast_add_fusion.x_ref, f32[4,512]{1,0:T(4,128)} %get-tuple-element.160.norm_ref, ...), custom_call_target="tpu_custom_call" | custom-call | flops 2684354560 | bytes 10485760 | tf_op jit(solution)/shard_map/attn_fwd/pallas_call | solution.py:240
  103.3 18.2 %mlp_fwd.2 = (f32[1024,512]{1,0:T(8,128)}, bf16[1024,2048]{1,0:T(8,128)(2,1)}, bf16[1024,2048]{1,0:T(8,128)(2,1)}) custom-call(s32[2]{0:T(128)} %pad_add_fusion.where_ref, f32[1024,512]{1,0:T(8,128)} %get-tuple-element.62.mid_ref, f32[4,512]{1,0:T(4,128)} %get-tuple-element.160.norm_ref, bf16[2,4,128,512]{3,2,1,0:T(8,128)(2,1)} %pad_maximum_fusion.refs_0_, ...), custom_call_target="tpu_custom_call" | custom-call | flops 4294967296 | bytes 12582912 | tf_op jit(solution)/shard_map/mlp_fwd/pallas_call | solution.py:299
  122.4 18.7 %attn_fwd.3 = (f32[1024,512]{1,0:T(8,128)}, bf16[1024,1536]{1,0:T(8,128)(2,1)}, bf16[4,8,256,256]{3,2,1,0:T(8,128)(2,1)}, bf16[4,512,256]{2,1,0:T(8,128)(2,1)}) custom-call(s32[2]{0:T(128)} %pad_add_fusion.where_ref, f32[1024,512]{1,0:T(8,128)} %get-tuple-element.63.x_ref, f32[4,512]{1,0:T(4,128)} %get-tuple-element.159.norm_ref, ...), custom_call_target="tpu_custom_call" | custom-call | flops 2684354560 | bytes 10485760 | tf_op jit(solution)/shard_map/attn_fwd/pallas_call | solution.py:240
  142.2 18.2 %mlp_fwd.3 = (f32[1024,512]{1,0:T(8,128)}, bf16[1024,2048]{1,0:T(8,128)(2,1)}, bf16[1024,2048]{1,0:T(8,128)(2,1)}) custom-call(s32[2]{0:T(128)} %pad_add_fusion.where_ref, f32[1024,512]{1,0:T(8,128)} %get-tuple-element.64.mid_ref, f32[4,512]{1,0:T(4,128)} %get-tuple-element.159.norm_ref, bf16[2,4,128,512]{3,2,1,0:T(8,128)(2,1)} %pad_maximum_fusion.1.refs_0_, ...), custom_call_target="tpu_custom_call" | custom-call | flops 4294967296 | bytes 12582912 | tf_op jit(solution)/shard_map/mlp_fwd/pallas_call | solution.py:299
  160.5 2.0 reduce_sum.121
  165.6 2.9 multiply_reduce_fusion
  170.7 2.4 fusion.84
  174.6 12.9 %mlp_bwd.2 = (f32[1024,512]{1,0:T(8,128)}, bf16[1024,2048]{1,0:T(8,128)(2,1)}, bf16[1024,512]{1,0:T(8,128)(2,1)}, bf16[1024,512]{1,0:T(8,128)(2,1)}, f32[8,512]{1,0:T(8,128)}) custom-call(s32[2]{0:T(128)} %pad_add_fusion.where_ref, f32[1024,512]{1,0:T(8,128)} %broadcast_add_fusion.dz_ref, f32[1024,512]{1,0:T(8,128)} %get-tuple-element.64.mid_ref, ...), custom_call_target="tpu_custom_call" | custom-call | flops 4294967296 | bytes 16777216 | tf_op jit(solution)/shard_map/mlp_bwd/pallas_call | solution.py:360
  187.5 28.6 %attn_bwd.2 = (f32[1024,512]{1,0:T(8,128)}, bf16[1024,1536]{1,0:T(8,128)(2,1)}, bf16[1024,512]{1,0:T(8,128)(2,1)}, bf16[1024,512]{1,0:T(8,128)(2,1)}, f32[8,512]{1,0:T(8,128)}) custom-call(s32[2]{0:T(128)} %pad_add_fusion.where_ref, f32[1024,512]{1,0:T(8,128)} %get-tuple-element.67.dmid_ref, f32[1024,512]{1,0:T(8,128)} %get-tuple-element.63.x_ref, ...), custom_call_target="tpu_custom_call" | custom-call | flops 3489660928 | bytes 16777216 | tf_op jit(solution)/shard_map/attn_bwd/pallas_call | solution.py:440
  216.1 12.9 %mlp_bwd.3 = (f32[1024,512]{1,0:T(8,128)}, bf16[1024,2048]{1,0:T(8,128)(2,1)}, bf16[1024,512]{1,0:T(8,128)(2,1)}, bf16[1024,512]{1,0:T(8,128)(2,1)}, f32[8,512]{1,0:T(8,128)}) custom-call(s32[2]{0:T(128)} %pad_add_fusion.where_ref, f32[1024,512]{1,0:T(8,128)} %get-tuple-element.71.dz_ref, f32[1024,512]{1,0:T(8,128)} %get-tuple-element.62.mid_ref, ...), custom_call_target="tpu_custom_call" | custom-call | flops 4294967296 | bytes 16777216 | tf_op jit(solution)/shard_map/mlp_bwd/pallas_call | solution.py:360
  229.0 17.3 %attn_bwd.3 = (f32[1024,512]{1,0:T(8,128)}, bf16[1024,1536]{1,0:T(8,128)(2,1)}, bf16[1024,512]{1,0:T(8,128)(2,1)}, bf16[1024,512]{1,0:T(8,128)(2,1)}, f32[8,512]{1,0:T(8,128)}) custom-call(s32[2]{0:T(128)} %pad_add_fusion.where_ref, f32[1024,512]{1,0:T(8,128)} %get-tuple-element.73.dmid_ref, f32[1024,512]{1,0:T(8,128)} %bitcast_add_fusion.x_ref, ...), custom_call_target="tpu_custom_call" | custom-call | flops 3489660928 | bytes 16777216 | tf_op jit(solution)/shard_map/attn_bwd/pallas_call | solution.py:440
  246.4 2.3 convolution_convert_fusion.1
  252.3 8.0 %grad_attn.3 = (bf16[4,2,128,512]{3,2,1,0:T(8,128)(2,1)}, bf16[4,2,128,512]{3,2,1,0:T(8,128)(2,1)}) custom-call(s32[2]{0:T(128)} %pad_add_fusion.where_ref, bf16[1024,512]{1,0:T(8,128)(2,1)} %get-tuple-element.93.a_ref, bf16[1024,1536]{1,0:T(8,128)(2,1)} %get-tuple-element.94.dqkv_ref, bf16[4,512,256]{2,1,0:T(8,128)(2,1)} %get-tuple-element.76.ot_ref, ...), custom_call_target="tpu_custom_call" | custom-call | flops 2147483648 | bytes 9437184 | tf_op jit(solution)/shard_map/grad_attn/pallas_call | solution.py:568
  264.8 14.9 %grad_mlp.2 = (bf16[4,4,128,512]{3,2,1,0:T(8,128)(2,1)}, bf16[4,4,128,512]{3,2,1,0:T(8,128)(2,1)}) custom-call(s32[2]{0:T(128)} %pad_add_fusion.where_ref, bf16[1024,512]{1,0:T(8,128)(2,1)} %get-tuple-element.87.c_ref, bf16[1024,2048]{1,0:T(8,128)(2,1)} %get-tuple-element.88.du_ref, bf16[1024,2048]{1,0:T(8,128)(2,1)} %get-tuple-element.89.act_ref, ...), custom_call_target="tpu_custom_call" | custom-call | flops 4294967296 | bytes 14680064 | tf_op jit(solution)/shard_map/grad_mlp/pallas_call | solution.py:507
  281.4 2.5 collective-permute-start.41
  284.0 8.0 %grad_attn.2 = (bf16[4,2,128,512]{3,2,1,0:T(8,128)(2,1)}, bf16[4,2,128,512]{3,2,1,0:T(8,128)(2,1)}) custom-call(s32[2]{0:T(128)} %pad_add_fusion.where_ref, bf16[1024,512]{1,0:T(8,128)(2,1)} %get-tuple-element.82.a_ref, bf16[1024,1536]{1,0:T(8,128)(2,1)} %get-tuple-element.83.dqkv_ref, bf16[4,512,256]{2,1,0:T(8,128)(2,1)} %get-tuple-element.70.ot_ref, ...), custom_call_target="tpu_custom_call" | custom-call | flops 2147483648 | bytes 9437184 | tf_op jit(solution)/shard_map/grad_attn/pallas_call | solution.py:568
  293.3 1.9 collective-permute-start.31
  297.5 3.2 collective-permute-start.32
  301.6 4.2 collective-permute-start.33
  306.9 1.8 collective-permute-start.34
  308.7 1.9 collective-permute-start.44
  310.5 1.7 collective-permute-start.43
  313.1 15.2 %grad_mlp.3 = (bf16[4,4,128,512]{3,2,1,0:T(8,128)(2,1)}, bf16[4,4,128,512]{3,2,1,0:T(8,128)(2,1)}) custom-call(s32[2]{0:T(128)} %pad_add_fusion.where_ref, bf16[1024,512]{1,0:T(8,128)(2,1)} %get-tuple-element.98.c_ref, bf16[1024,2048]{1,0:T(8,128)(2,1)} %get-tuple-element.99.du_ref, bf16[1024,2048]{1,0:T(8,128)(2,1)} %get-tuple-element.100.act_ref, ...), custom_call_target="tpu_custom_call" | custom-call | flops 4294967296 | bytes 14680064 | tf_op jit(solution)/shard_map/grad_mlp/pallas_call | solution.py:507
  336.1 3.7 collective-permute-done.66
  340.3 5.1 collective-permute-done.68
  348.4 2.7 collective-permute-done.46
  352.0 3.9 collective-permute-done.48
  355.8 2.9 collective-permute-start.71
  358.7 1.7 collective-permute-done.47
  360.4 1.9 collective-permute-start.70
  367.8 4.3 collective-permute-start.74
  374.1 2.7 collective-permute-start.72
  376.9 2.0 collective-permute-done.73
  380.6 2.4 collective-permute-start.52
  384.2 2.5 collective-permute-done.52
  391.1 2.0 fusion.16
  396.8 1.8 fusion.12
  400.6 7.3 %collective-permute-done.76 = bf16[4,128,512]{2,1,0:T(8,128)(2,1)S(1)} collective-permute-done((bf16[4,128,512]{2,1,0:T(8,128)(2,1)S(1)}, bf16[4,128,512]{2,1,0:T(8,128)(2,1)S(1)}, u32[]{:S(2)}, u32[]{:S(2)}) %collective-permute-start.76) | collective-permute-done | bytes 524320 | tf_op jit(solution)/shard_map/ppermute | solution.py:67
  409.1 9.9 %collective-permute-done.78 = bf16[4,128,512]{2,1,0:T(8,128)(2,1)S(1)} collective-permute-done((bf16[4,128,512]{2,1,0:T(8,128)(2,1)S(1)}, bf16[4,128,512]{2,1,0:T(8,128)(2,1)S(1)}, u32[]{:S(2)}, u32[]{:S(2)}) %collective-permute-start.78) | collective-permute-done | bytes 524320 | tf_op jit(solution)/shard_map/ppermute | solution.py:67
  419.0 2.1 collective-permute-done.77
  422.9 2.7 collective-permute-start.81
  425.6 4.8 collective-permute-done.56
  430.4 10.6 %collective-permute-done.58 = bf16[4,128,512]{2,1,0:T(8,128)(2,1)S(1)} collective-permute-done((bf16[4,128,512]{2,1,0:T(8,128)(2,1)S(1)}, bf16[4,128,512]{2,1,0:T(8,128)(2,1)S(1)}, u32[]{:S(2)}, u32[]{:S(2)}) %collective-permute-start.58) | collective-permute-done | bytes 524320 | tf_op jit(solution)/shard_map/ppermute | solution.py:67
  444.5 2.4 collective-permute-start.61
  449.1 2.0 collective-permute-start.83
  452.0 3.9 collective-permute-start.82
  455.9 12.0 %collective-permute-done.60 = bf16[128,512]{1,0:T(8,128)(2,1)S(1)} collective-permute-done((bf16[128,512]{1,0:T(8,128)(2,1)S(1)}, bf16[128,512]{1,0:T(8,128)(2,1)S(1)}, u32[]{:S(2)}, u32[]{:S(2)}) %collective-permute-start.60) | collective-permute-done | bytes 131104 | tf_op jit(solution)/shard_map/ppermute | solution.py:67
  468.1 3.4 collective-permute-start.63
  474.3 4.9 collective-permute-done.63
  484.2 2.8 collective-permute-start.88
  487.0 2.7 collective-permute-start.87
  489.7 1.9 collective-permute-start.86
  491.7 1.7 collective-permute-done.86
  495.4 1.9 multiply_subtract_fusion.4
  497.4 5.1 multiply_subtract_fusion.2
  509.8 4.1 multiply_subtract_fusion
  514.6 3.9 multiply_subtract_fusion.1
  (370 shorter events, 110.2 us)
Async XLA Ops:
  2.6 20.2 %collective-permute-start.4 = (f32[200,128]{1,0:T(8,128)}, f32[200,128]{1,0:T(8,128)S(1)}, u32[]{:S(2)}, u32[]{:S(2)}) collective-permute-start(f32[200,128]{1,0:T(8,128)} %dynamic-slice_bitcast_fusion.8), channel_id=1, source_target_pairs={{0,8},{8,0},{16,24},{24,16},{1,9},{9,1},{17,25},{25,17},{2,10},{10... | collective-permute-start | bytes 307208 | tf_op jit(solution)/shard_map/ppermute | solution.py:67
  5.5 18.4 %collective-permute-start.2 = (f32[200,128]{1,0:T(8,128)}, f32[200,128]{1,0:T(8,128)}, u32[]{:S(2)}, u32[]{:S(2)}) collective-permute-start(f32[200,128]{1,0:T(8,128)} %dynamic-slice_bitcast_fusion.8), channel_id=1, source_target_pairs={{0,16},{8,24},{16,0},{24,8},{1,17},{9,25},{17,1},{25,9},{2,18},{10... | collective-permute-start | bytes 307208 | tf_op jit(solution)/shard_map/ppermute | solution.py:67
  7.1 17.0 %collective-permute-start = (f32[200,128]{1,0:T(8,128)}, f32[200,128]{1,0:T(8,128)S(1)}, u32[]{:S(2)}, u32[]{:S(2)}) collective-permute-start(f32[200,128]{1,0:T(8,128)} %dynamic-slice_bitcast_fusion.8), channel_id=1, source_target_pairs={{0,24},{8,16},{16,8},{24,0},{1,25},{9,17},{17,9},{25,1},{2,26},{10... | collective-permute-start | bytes 307208 | tf_op jit(solution)/shard_map/ppermute | solution.py:67
  10.7 19.8 %collective-permute-start.8 = (bf16[2,128,512]{2,1,0:T(8,128)(2,1)}, bf16[2,128,512]{2,1,0:T(8,128)(2,1)}, u32[]{:S(2)}, u32[]{:S(2)}) collective-permute-start(bf16[2,128,512]{2,1,0:T(8,128)(2,1)} %dynamic-slice_bitcast_fusion.1), channel_id=1, source_target_pairs={{0,24},{8,16},{16,8},{24,0},{1,25},{9,17},{17,9},{25,1},{2,26},{10... | collective-permute-start | bytes 786440 | tf_op jit(solution)/shard_map/ppermute | solution.py:67
  13.6 17.6 %collective-permute-start.7 = (bf16[2,128,512]{2,1,0:T(8,128)(2,1)}, bf16[2,128,512]{2,1,0:T(8,128)(2,1)}, u32[]{:S(2)}, u32[]{:S(2)}) collective-permute-start(bf16[2,128,512]{2,1,0:T(8,128)(2,1)} %dynamic-slice_bitcast_fusion.1), channel_id=1, source_target_pairs={{0,16},{8,24},{16,0},{24,8},{1,17},{9,25},{17,1},{25,9},{2,18},{10... | collective-permute-start | bytes 786440 | tf_op jit(solution)/shard_map/ppermute | solution.py:67
  25.3 12.2 %collective-permute-start.20 = (bf16[2,128,512]{2,1,0:T(8,128)(2,1)S(1)}, bf16[2,128,512]{2,1,0:T(8,128)(2,1)S(1)}, u32[]{:S(2)}, u32[]{:S(2)}) collective-permute-start(bf16[2,128,512]{2,1,0:T(8,128)(2,1)S(1)} %dynamic-slice_bitcast_fusion), channel_id=1, source_target_pairs={{0,24},{8,16},{16,8},{24,0},{1,25},{9,17},{17,9},{25,1},{2,26},{10... | collective-permute-start | bytes 786440 | tf_op jit(solution)/shard_map/ppermute | solution.py:67
  29.9 11.9 %collective-permute-start.19 = (bf16[2,128,512]{2,1,0:T(8,128)(2,1)S(1)}, bf16[2,128,512]{2,1,0:T(8,128)(2,1)S(1)}, u32[]{:S(2)}, u32[]{:S(2)}) collective-permute-start(bf16[2,128,512]{2,1,0:T(8,128)(2,1)S(1)} %dynamic-slice_bitcast_fusion), channel_id=1, source_target_pairs={{0,16},{8,24},{16,0},{24,8},{1,17},{9,25},{17,1},{25,9},{2,18},{10... | collective-permute-start | bytes 786440 | tf_op jit(solution)/shard_map/ppermute | solution.py:67
  30.5 12.7 %collective-permute-start.18 = (bf16[2,128,512]{2,1,0:T(8,128)(2,1)S(1)}, bf16[2,128,512]{2,1,0:T(8,128)(2,1)S(1)}, u32[]{:S(2)}, u32[]{:S(2)}) collective-permute-start(bf16[2,128,512]{2,1,0:T(8,128)(2,1)S(1)} %dynamic-slice_bitcast_fusion), channel_id=1, source_target_pairs={{0,8},{8,0},{16,24},{24,16},{1,9},{9,1},{17,25},{25,17},{2,10},{10... | collective-permute-start | bytes 786440 | tf_op jit(solution)/shard_map/ppermute | solution.py:67
  31.2 12.6 %collective-permute-start.11 = (bf16[2,128,512]{2,1,0:T(8,128)(2,1)}, bf16[2,128,512]{2,1,0:T(8,128)(2,1)S(1)}, u32[]{:S(2)}, u32[]{:S(2)}) collective-permute-start(bf16[2,128,512]{2,1,0:T(8,128)(2,1)} %collective-permute-done.8.refs_3_), channel_id=1, source_target_pairs={{0,1},{1,0},{2,3},{3,2},{4,5},{5,4},{6,7},{7,6},{8,9},{9,8},{10,11... | collective-permute-start | bytes 786440 | tf_op jit(solution)/shard_map/ppermute | solution.py:67
  31.2 14.1 %collective-permute-start.10 = (bf16[2,128,512]{2,1,0:T(8,128)(2,1)}, bf16[2,128,512]{2,1,0:T(8,128)(2,1)S(1)}, u32[]{:S(2)}, u32[]{:S(2)}) collective-permute-start(bf16[2,128,512]{2,1,0:T(8,128)(2,1)} %collective-permute-done.7.refs_2_), channel_id=1, source_target_pairs={{0,1},{1,0},{2,3},{3,2},{4,5},{5,4},{6,7},{7,6},{8,9},{9,8},{10,11... | collective-permute-start | bytes 786440 | tf_op jit(solution)/shard_map/ppermute | solution.py:67
  37.6 9.4 %collective-permute-start.9 = (bf16[2,128,512]{2,1,0:T(8,128)(2,1)}, bf16[2,128,512]{2,1,0:T(8,128)(2,1)S(1)}, u32[]{:S(2)}, u32[]{:S(2)}) collective-permute-start(bf16[2,128,512]{2,1,0:T(8,128)(2,1)} %collective-permute-done.6.refs_1_), channel_id=1, source_target_pairs={{0,1},{1,0},{2,3},{3,2},{4,5},{5,4},{6,7},{7,6},{8,9},{9,8},{10,11... | collective-permute-start | bytes 786440 | tf_op jit(solution)/shard_map/ppermute | solution.py:67
  41.8 38.2 %collective-permute-start.14 = (bf16[4,128,512]{2,1,0:T(8,128)(2,1)}, bf16[4,128,512]{2,1,0:T(8,128)(2,1)}, u32[]{:S(2)}, u32[]{:S(2)}) collective-permute-start(bf16[4,128,512]{2,1,0:T(8,128)(2,1)} %fusion.22), channel_id=1, source_target_pairs={{0,24},{8,16},{16,8},{24,0},{1,25},{9,17},{17,9},{25,1},{2,26},{10... | collective-permute-start | bytes 1572872 | tf_op jit(solution)/shard_map/ppermute | solution.py:67
  43.1 36.9 %collective-permute-start.13 = (bf16[4,128,512]{2,1,0:T(8,128)(2,1)}, bf16[4,128,512]{2,1,0:T(8,128)(2,1)}, u32[]{:S(2)}, u32[]{:S(2)}) collective-permute-start(bf16[4,128,512]{2,1,0:T(8,128)(2,1)} %fusion.22), channel_id=1, source_target_pairs={{0,16},{8,24},{16,0},{24,8},{1,17},{9,25},{17,1},{25,9},{2,18},{10... | collective-permute-start | bytes 1572872 | tf_op jit(solution)/shard_map/ppermute | solution.py:67
  43.9 36.7 %collective-permute-start.12 = (bf16[4,128,512]{2,1,0:T(8,128)(2,1)}, bf16[4,128,512]{2,1,0:T(8,128)(2,1)}, u32[]{:S(2)}, u32[]{:S(2)}) collective-permute-start(bf16[4,128,512]{2,1,0:T(8,128)(2,1)} %fusion.22), channel_id=1, source_target_pairs={{0,8},{8,0},{16,24},{24,16},{1,9},{9,1},{17,25},{25,17},{2,10},{10... | collective-permute-start | bytes 1572872 | tf_op jit(solution)/shard_map/ppermute | solution.py:67
  45.4 34.1 %collective-permute-start.26 = (bf16[4,128,512]{2,1,0:T(8,128)(2,1)}, bf16[4,128,512]{2,1,0:T(8,128)(2,1)S(1)}, u32[]{:S(2)}, u32[]{:S(2)}) collective-permute-start(bf16[4,128,512]{2,1,0:T(8,128)(2,1)} %fusion.20), channel_id=1, source_target_pairs={{0,24},{8,16},{16,8},{24,0},{1,25},{9,17},{17,9},{25,1},{2,26},{10... | collective-permute-start | bytes 1572872 | tf_op jit(solution)/shard_map/ppermute | solution.py:67
  48.5 53.2 %collective-permute-start.25 = (bf16[4,128,512]{2,1,0:T(8,128)(2,1)}, bf16[4,128,512]{2,1,0:T(8,128)(2,1)}, u32[]{:S(2)}, u32[]{:S(2)}) collective-permute-start(bf16[4,128,512]{2,1,0:T(8,128)(2,1)} %fusion.20), channel_id=1, source_target_pairs={{0,16},{8,24},{16,0},{24,8},{1,17},{9,25},{17,1},{25,9},{2,18},{10... | collective-permute-start | bytes 1572872 | tf_op jit(solution)/shard_map/ppermute | solution.py:67
  79.5 22.8 %collective-permute-start.24 = (bf16[4,128,512]{2,1,0:T(8,128)(2,1)}, bf16[4,128,512]{2,1,0:T(8,128)(2,1)}, u32[]{:S(2)}, u32[]{:S(2)}) collective-permute-start(bf16[4,128,512]{2,1,0:T(8,128)(2,1)} %fusion.20), channel_id=1, source_target_pairs={{0,8},{8,0},{16,24},{24,16},{1,9},{9,1},{17,25},{25,17},{2,10},{10... | collective-permute-start | bytes 1572872 | tf_op jit(solution)/shard_map/ppermute | solution.py:67
  80.0 22.4 %collective-permute-start.17 = (bf16[4,128,512]{2,1,0:T(8,128)(2,1)}, bf16[4,128,512]{2,1,0:T(8,128)(2,1)}, u32[]{:S(2)}, u32[]{:S(2)}) collective-permute-start(bf16[4,128,512]{2,1,0:T(8,128)(2,1)} %collective-permute-done.14.refs_3_), channel_id=1, source_target_pairs={{0,1},{1,0},{2,3},{3,2},{4,5},{5,4},{6,7},{7,6},{8,9},{9,8},{10,11... | collective-permute-start | bytes 1572872 | tf_op jit(solution)/shard_map/ppermute | solution.py:67
  80.0 22.8 %collective-permute-start.16 = (bf16[4,128,512]{2,1,0:T(8,128)(2,1)}, bf16[4,128,512]{2,1,0:T(8,128)(2,1)}, u32[]{:S(2)}, u32[]{:S(2)}) collective-permute-start(bf16[4,128,512]{2,1,0:T(8,128)(2,1)} %collective-permute-done.13.refs_2_), channel_id=1, source_target_pairs={{0,1},{1,0},{2,3},{3,2},{4,5},{5,4},{6,7},{7,6},{8,9},{9,8},{10,11... | collective-permute-start | bytes 1572872 | tf_op jit(solution)/shard_map/ppermute | solution.py:67
  80.5 22.4 %collective-permute-start.15 = (bf16[4,128,512]{2,1,0:T(8,128)(2,1)}, bf16[4,128,512]{2,1,0:T(8,128)(2,1)}, u32[]{:S(2)}, u32[]{:S(2)}) collective-permute-start(bf16[4,128,512]{2,1,0:T(8,128)(2,1)} %collective-permute-done.12.refs_1_), channel_id=1, source_target_pairs={{0,1},{1,0},{2,3},{3,2},{4,5},{5,4},{6,7},{7,6},{8,9},{9,8},{10,11... | collective-permute-start | bytes 1572872 | tf_op jit(solution)/shard_map/ppermute | solution.py:67
  101.8 19.8 %collective-permute-start.22 = (bf16[2,128,512]{2,1,0:T(8,128)(2,1)S(1)}, bf16[2,128,512]{2,1,0:T(8,128)(2,1)S(1)}, u32[]{:S(2)}, u32[]{:S(2)}) collective-permute-start(bf16[2,128,512]{2,1,0:T(8,128)(2,1)S(1)} %copy-done.30), channel_id=1, source_target_pairs={{0,1},{1,0},{2,3},{3,2},{4,5},{5,4},{6,7},{7,6},{8,9},{9,8},{10,11... | collective-permute-start | bytes 786440 | tf_op jit(solution)/shard_map/ppermute | solution.py:67
  102.3 19.3 %collective-permute-start.21 = (bf16[2,128,512]{2,1,0:T(8,128)(2,1)S(1)}, bf16[2,128,512]{2,1,0:T(8,128)(2,1)S(1)}, u32[]{:S(2)}, u32[]{:S(2)}) collective-permute-start(bf16[2,128,512]{2,1,0:T(8,128)(2,1)S(1)} %copy-done.32), channel_id=1, source_target_pairs={{0,1},{1,0},{2,3},{3,2},{4,5},{5,4},{6,7},{7,6},{8,9},{9,8},{10,11... | collective-permute-start | bytes 786440 | tf_op jit(solution)/shard_map/ppermute | solution.py:67
  102.4 38.7 %collective-permute-start.29 = (bf16[4,128,512]{2,1,0:T(8,128)(2,1)S(1)}, bf16[4,128,512]{2,1,0:T(8,128)(2,1)S(1)}, u32[]{:S(2)}, u32[]{:S(2)}) collective-permute-start(bf16[4,128,512]{2,1,0:T(8,128)(2,1)S(1)} %copy-done.49), channel_id=1, source_target_pairs={{0,1},{1,0},{2,3},{3,2},{4,5},{5,4},{6,7},{7,6},{8,9},{9,8},{10,11... | collective-permute-start | bytes 1572872 | tf_op jit(solution)/shard_map/ppermute | solution.py:67
  102.8 38.3 %collective-permute-start.28 = (bf16[4,128,512]{2,1,0:T(8,128)(2,1)}, bf16[4,128,512]{2,1,0:T(8,128)(2,1)S(1)}, u32[]{:S(2)}, u32[]{:S(2)}) collective-permute-start(bf16[4,128,512]{2,1,0:T(8,128)(2,1)} %collective-permute-done.25.refs_2_), channel_id=1, source_target_pairs={{0,1},{1,0},{2,3},{3,2},{4,5},{5,4},{6,7},{7,6},{8,9},{9,8},{10,11... | collective-permute-start | bytes 1572872 | tf_op jit(solution)/shard_map/ppermute | solution.py:67
  102.9 38.2 %collective-permute-start.27 = (bf16[4,128,512]{2,1,0:T(8,128)(2,1)}, bf16[4,128,512]{2,1,0:T(8,128)(2,1)S(1)}, u32[]{:S(2)}, u32[]{:S(2)}) collective-permute-start(bf16[4,128,512]{2,1,0:T(8,128)(2,1)} %collective-permute-done.24.refs_1_), channel_id=1, source_target_pairs={{0,1},{1,0},{2,3},{3,2},{4,5},{5,4},{6,7},{7,6},{8,9},{9,8},{10,11... | collective-permute-start | bytes 1572872 | tf_op jit(solution)/shard_map/ppermute | solution.py:67
  169.2 122.8 %collective-permute-start.30 = (f32[1,1]{1,0:T(1,128)}, f32[1,1]{1,0:T(1,128)}, u32[]{:S(2)}, u32[]{:S(2)}) collective-permute-start(f32[1,1]{1,0:T(1,128)} %bitcast.32), channel_id=1, source_target_pairs={{0,8},{8,0},{16,24},{24,16},{1,9},{9,1},{17,25},{25,17},{2,10},{10... | collective-permute-start | bytes 20 | tf_op jit(solution)/shard_map/ppermute | solution.py:67
  260.3 70.0 %collective-permute-start.65 = (bf16[4,2,128,512]{3,2,1,0:T(8,128)(2,1)}, bf16[4,2,128,512]{3,2,1,0:T(8,128)(2,1)S(1)}, u32[]{:S(2)}, u32[]{:S(2)}) collective-permute-start(bf16[4,2,128,512]{3,2,1,0:T(8,128)(2,1)} %get-tuple-element.97), channel_id=1, source_target_pairs={{0,1},{1,0},{2,3},{3,2},{4,5},{5,4},{6,7},{7,6},{8,9},{9,8},{10,11... | collective-permute-start | bytes 3145736 | tf_op jit(solution)/shard_map/ppermute | solution.py:67
  261.2 18.4 %collective-permute-start.36 = (bf16[200,128]{1,0:T(8,128)(2,1)S(1)}, bf16[200,128]{1,0:T(8,128)(2,1)S(1)}, u32[]{:S(2)}, u32[]{:S(2)}) collective-permute-start(bf16[200,128]{1,0:T(8,128)(2,1)S(1)} %get-tuple-element.221), channel_id=1, source_target_pairs={{0,8},{8,0},{16,24},{24,16},{1,9},{9,1},{17,25},{25,17},{2,10},{10... | collective-permute-start | bytes 153608 | tf_op jit(solution)/shard_map/ppermute | solution.py:67
  261.8 17.8 %collective-permute-start.38 = (bf16[200,128]{1,0:T(8,128)(2,1)S(1)}, bf16[200,128]{1,0:T(8,128)(2,1)S(1)}, u32[]{:S(2)}, u32[]{:S(2)}) collective-permute-start(bf16[200,128]{1,0:T(8,128)(2,1)S(1)} %get-tuple-element.222), channel_id=1, source_target_pairs={{0,24},{8,16},{16,8},{24,0},{1,25},{9,17},{17,9},{25,1},{2,26},{10... | collective-permute-start | bytes 153608 | tf_op jit(solution)/shard_map/ppermute | solution.py:67
  263.2 16.4 %collective-permute-start.37 = (bf16[200,128]{1,0:T(8,128)(2,1)S(1)}, bf16[200,128]{1,0:T(8,128)(2,1)S(1)}, u32[]{:S(2)}, u32[]{:S(2)}) collective-permute-start(bf16[200,128]{1,0:T(8,128)(2,1)S(1)} %get-tuple-element.223), channel_id=1, source_target_pairs={{0,16},{8,24},{16,0},{24,8},{1,17},{9,25},{17,1},{25,9},{2,18},{10... | collective-permute-start | bytes 153608 | tf_op jit(solution)/shard_map/ppermute | solution.py:67
  279.7 27.2 %collective-permute-start.39 = (bf16[56,128]{1,0:T(8,128)(2,1)S(1)}, bf16[56,128]{1,0:T(8,128)(2,1)S(1)}, u32[]{:S(2)}, u32[]{:S(2)}) collective-permute-start(bf16[56,128]{1,0:T(8,128)(2,1)S(1)} %get-tuple-element.230), channel_id=1, source_target_pairs={{0,2},{1,3},{2,0},{3,1},{4,6},{5,7},{6,4},{7,5},{8,10},{9,11},{10,... | collective-permute-start | bytes 43016 | tf_op jit(solution)/shard_map/ppermute | solution.py:67
  281.4 27.3 %collective-permute-start.41 = (bf16[56,128]{1,0:T(8,128)(2,1)S(1)}, bf16[56,128]{1,0:T(8,128)(2,1)S(1)}, u32[]{:S(2)}, u32[]{:S(2)}) collective-permute-start(bf16[56,128]{1,0:T(8,128)(2,1)S(1)} %get-tuple-element.231), channel_id=1, source_target_pairs={{0,6},{1,7},{2,4},{3,5},{4,2},{5,3},{6,0},{7,1},{8,14},{9,15},{10,... | collective-permute-start | bytes 43016 | tf_op jit(solution)/shard_map/ppermute | solution.py:67
  283.8 24.8 %collective-permute-start.40 = (bf16[56,128]{1,0:T(8,128)(2,1)S(1)}, bf16[56,128]{1,0:T(8,128)(2,1)S(1)}, u32[]{:S(2)}, u32[]{:S(2)}) collective-permute-start(bf16[56,128]{1,0:T(8,128)(2,1)S(1)} %get-tuple-element.232), channel_id=1, source_target_pairs={{0,4},{1,5},{2,6},{3,7},{4,0},{5,1},{6,2},{7,3},{8,12},{9,13},{10,... | collective-permute-start | bytes 43016 | tf_op jit(solution)/shard_map/ppermute | solution.py:67
  306.2 28.5 %collective-permute-start.45 = (bf16[4,2,128,512]{3,2,1,0:T(8,128)(2,1)}, bf16[4,2,128,512]{3,2,1,0:T(8,128)(2,1)}, u32[]{:S(2)}, u32[]{:S(2)}) collective-permute-start(bf16[4,2,128,512]{3,2,1,0:T(8,128)(2,1)} %get-tuple-element.86), channel_id=1, source_target_pairs={{0,1},{1,0},{2,3},{3,2},{4,5},{5,4},{6,7},{7,6},{8,9},{9,8},{10,11... | collective-permute-start | bytes 3145736 | tf_op jit(solution)/shard_map/ppermute | solution.py:67
  308.7 20.4 %collective-permute-start.44 = (bf16[56,128]{1,0:T(8,128)(2,1)S(1)}, bf16[56,128]{1,0:T(8,128)(2,1)S(1)}, u32[]{:S(2)}, u32[]{:S(2)}) collective-permute-start(bf16[56,128]{1,0:T(8,128)(2,1)S(1)} %fusion.68), channel_id=1, source_target_pairs={{0,2},{1,3},{2,0},{3,1},{4,6},{5,7},{6,4},{7,5},{8,10},{9,11},{10,... | collective-permute-start | bytes 43016 | tf_op jit(solution)/shard_map/ppermute | solution.py:67
  310.5 18.6 %collective-permute-start.43 = (bf16[56,128]{1,0:T(8,128)(2,1)S(1)}, bf16[56,128]{1,0:T(8,128)(2,1)S(1)}, u32[]{:S(2)}, u32[]{:S(2)}) collective-permute-start(bf16[56,128]{1,0:T(8,128)(2,1)S(1)} %fusion.68), channel_id=1, source_target_pairs={{0,4},{1,5},{2,6},{3,7},{4,0},{5,1},{6,2},{7,3},{8,12},{9,13},{10,... | collective-permute-start | bytes 43016 | tf_op jit(solution)/shard_map/ppermute | solution.py:67
  312.2 16.9 %collective-permute-start.42 = (bf16[56,128]{1,0:T(8,128)(2,1)S(1)}, bf16[56,128]{1,0:T(8,128)(2,1)S(1)}, u32[]{:S(2)}, u32[]{:S(2)}) collective-permute-start(bf16[56,128]{1,0:T(8,128)(2,1)S(1)} %fusion.68), channel_id=1, source_target_pairs={{0,6},{1,7},{2,4},{3,5},{4,2},{5,3},{6,0},{7,1},{8,14},{9,15},{10,... | collective-permute-start | bytes 43016 | tf_op jit(solution)/shard_map/ppermute | solution.py:67
  329.1 62.0 %collective-permute-start.75 = (bf16[4,4,128,512]{3,2,1,0:T(8,128)(2,1)}, bf16[4,4,128,512]{3,2,1,0:T(8,128)(2,1)}, u32[]{:S(2)}, u32[]{:S(2)}) collective-permute-start(bf16[4,4,128,512]{3,2,1,0:T(8,128)(2,1)} %get-tuple-element.103), channel_id=1, source_target_pairs={{0,1},{1,0},{2,3},{3,2},{4,5},{5,4},{6,7},{7,6},{8,9},{9,8},{10,11... | collective-permute-start | bytes 6291464 | tf_op jit(solution)/shard_map/ppermute | solution.py:67
  331.2 14.2 %collective-permute-start.68 = (bf16[2,128,512]{2,1,0:T(8,128)(2,1)S(1)}, bf16[2,128,512]{2,1,0:T(8,128)(2,1)S(1)}, u32[]{:S(2)}, u32[]{:S(2)}) collective-permute-start(bf16[2,128,512]{2,1,0:T(8,128)(2,1)S(1)} %get-tuple-element.144), channel_id=1, source_target_pairs={{0,24},{8,16},{16,8},{24,0},{1,25},{9,17},{17,9},{25,1},{2,26},{10... | collective-permute-start | bytes 786440 | tf_op jit(solution)/shard_map/ppermute | solution.py:67
  333.4 14.0 %collective-permute-start.67 = (bf16[2,128,512]{2,1,0:T(8,128)(2,1)S(1)}, bf16[2,128,512]{2,1,0:T(8,128)(2,1)S(1)}, u32[]{:S(2)}, u32[]{:S(2)}) collective-permute-start(bf16[2,128,512]{2,1,0:T(8,128)(2,1)S(1)} %get-tuple-element.145), channel_id=1, source_target_pairs={{0,16},{8,24},{16,0},{24,8},{1,17},{9,25},{17,1},{25,9},{2,18},{10... | collective-permute-start | bytes 786440 | tf_op jit(solution)/shard_map/ppermute | solution.py:67
  334.8 62.0 %collective-permute-start.55 = (bf16[4,4,128,512]{3,2,1,0:T(8,128)(2,1)}, bf16[4,4,128,512]{3,2,1,0:T(8,128)(2,1)}, u32[]{:S(2)}, u32[]{:S(2)}) collective-permute-start(bf16[4,4,128,512]{3,2,1,0:T(8,128)(2,1)} %get-tuple-element.92), channel_id=1, source_target_pairs={{0,1},{1,0},{2,3},{3,2},{4,5},{5,4},{6,7},{7,6},{8,9},{9,8},{10,11... | collective-permute-start | bytes 6291464 | tf_op jit(solution)/shard_map/ppermute | solution.py:67
  339.8 11.3 %collective-permute-start.46 = (bf16[2,128,512]{2,1,0:T(8,128)(2,1)S(1)}, bf16[2,128,512]{2,1,0:T(8,128)(2,1)S(1)}, u32[]{:S(2)}, u32[]{:S(2)}) collective-permute-start(bf16[2,128,512]{2,1,0:T(8,128)(2,1)S(1)} %get-tuple-element.146), channel_id=1, source_target_pairs={{0,8},{8,0},{16,24},{24,16},{1,9},{9,1},{17,25},{25,17},{2,10},{10... | collective-permute-start | bytes 786440 | tf_op jit(solution)/shard_map/ppermute | solution.py:67
  345.4 10.4 %collective-permute-start.48 = (bf16[2,128,512]{2,1,0:T(8,128)(2,1)S(1)}, bf16[2,128,512]{2,1,0:T(8,128)(2,1)S(1)}, u32[]{:S(2)}, u32[]{:S(2)}) collective-permute-start(bf16[2,128,512]{2,1,0:T(8,128)(2,1)S(1)} %get-tuple-element.147), channel_id=1, source_target_pairs={{0,24},{8,16},{16,8},{24,0},{1,25},{9,17},{17,9},{25,1},{2,26},{10... | collective-permute-start | bytes 786440 | tf_op jit(solution)/shard_map/ppermute | solution.py:67
  347.3 13.1 %collective-permute-start.47 = (bf16[2,128,512]{2,1,0:T(8,128)(2,1)S(1)}, bf16[2,128,512]{2,1,0:T(8,128)(2,1)S(1)}, u32[]{:S(2)}, u32[]{:S(2)}) collective-permute-start(bf16[2,128,512]{2,1,0:T(8,128)(2,1)S(1)} %get-tuple-element.148), channel_id=1, source_target_pairs={{0,16},{8,24},{16,0},{24,8},{1,17},{9,25},{17,1},{25,9},{2,18},{10... | collective-permute-start | bytes 786440 | tf_op jit(solution)/shard_map/ppermute | solution.py:67
  351.1 12.4 %collective-permute-start.69 = (bf16[64,512]{1,0:T(8,128)(2,1)S(1)}, bf16[64,512]{1,0:T(8,128)(2,1)S(1)}, u32[]{:S(2)}, u32[]{:S(2)}) collective-permute-start(bf16[64,512]{1,0:T(8,128)(2,1)S(1)} %get-tuple-element.209), channel_id=1, source_target_pairs={{0,2},{1,3},{2,0},{3,1},{4,6},{5,7},{6,4},{7,5},{8,10},{9,11},{10,... | collective-permute-start | bytes 196616 | tf_op jit(solution)/shard_map/ppermute | solution.py:67
  355.8 9.3 %collective-permute-start.71 = (bf16[64,512]{1,0:T(8,128)(2,1)S(1)}, bf16[64,512]{1,0:T(8,128)(2,1)S(1)}, u32[]{:S(2)}, u32[]{:S(2)}) collective-permute-start(bf16[64,512]{1,0:T(8,128)(2,1)S(1)} %get-tuple-element.210), channel_id=1, source_target_pairs={{0,6},{1,7},{2,4},{3,5},{4,2},{5,3},{6,0},{7,1},{8,14},{9,15},{10,... | collective-permute-start | bytes 196616 | tf_op jit(solution)/shard_map/ppermute | solution.py:67
  393.1 14.8 %collective-permute-start.76 = (bf16[4,128,512]{2,1,0:T(8,128)(2,1)S(1)}, bf16[4,128,512]{2,1,0:T(8,128)(2,1)S(1)}, u32[]{:S(2)}, u32[]{:S(2)}) collective-permute-start(bf16[4,128,512]{2,1,0:T(8,128)(2,1)S(1)} %get-tuple-element.137), channel_id=1, source_target_pairs={{0,8},{8,0},{16,24},{24,16},{1,9},{9,1},{17,25},{25,17},{2,10},{10... | collective-permute-start | bytes 1572872 | tf_op jit(solution)/shard_map/ppermute | solution.py:67
  393.9 25.2 %collective-permute-start.78 = (bf16[4,128,512]{2,1,0:T(8,128)(2,1)S(1)}, bf16[4,128,512]{2,1,0:T(8,128)(2,1)S(1)}, u32[]{:S(2)}, u32[]{:S(2)}) collective-permute-start(bf16[4,128,512]{2,1,0:T(8,128)(2,1)S(1)} %get-tuple-element.138), channel_id=1, source_target_pairs={{0,24},{8,16},{16,8},{24,0},{1,25},{9,17},{17,9},{25,1},{2,26},{10... | collective-permute-start | bytes 1572872 | tf_op jit(solution)/shard_map/ppermute | solution.py:67
  395.1 26.1 %collective-permute-start.77 = (bf16[4,128,512]{2,1,0:T(8,128)(2,1)S(1)}, bf16[4,128,512]{2,1,0:T(8,128)(2,1)S(1)}, u32[]{:S(2)}, u32[]{:S(2)}) collective-permute-start(bf16[4,128,512]{2,1,0:T(8,128)(2,1)S(1)} %get-tuple-element.139), channel_id=1, source_target_pairs={{0,16},{8,24},{16,0},{24,8},{1,17},{9,25},{17,1},{25,9},{2,18},{10... | collective-permute-start | bytes 1572872 | tf_op jit(solution)/shard_map/ppermute | solution.py:67
  398.6 31.8 %collective-permute-start.56 = (bf16[4,128,512]{2,1,0:T(8,128)(2,1)S(1)}, bf16[4,128,512]{2,1,0:T(8,128)(2,1)S(1)}, u32[]{:S(2)}, u32[]{:S(2)}) collective-permute-start(bf16[4,128,512]{2,1,0:T(8,128)(2,1)S(1)} %get-tuple-element.140), channel_id=1, source_target_pairs={{0,8},{8,0},{16,24},{24,16},{1,9},{9,1},{17,25},{25,17},{2,10},{10... | collective-permute-start | bytes 1572872 | tf_op jit(solution)/shard_map/ppermute | solution.py:67
  399.4 41.7 %collective-permute-start.58 = (bf16[4,128,512]{2,1,0:T(8,128)(2,1)S(1)}, bf16[4,128,512]{2,1,0:T(8,128)(2,1)S(1)}, u32[]{:S(2)}, u32[]{:S(2)}) collective-permute-start(bf16[4,128,512]{2,1,0:T(8,128)(2,1)S(1)} %get-tuple-element.141), channel_id=1, source_target_pairs={{0,24},{8,16},{16,8},{24,0},{1,25},{9,17},{17,9},{25,1},{2,26},{10... | collective-permute-start | bytes 1572872 | tf_op jit(solution)/shard_map/ppermute | solution.py:67
  407.9 34.6 %collective-permute-start.57 = (bf16[4,128,512]{2,1,0:T(8,128)(2,1)S(1)}, bf16[4,128,512]{2,1,0:T(8,128)(2,1)S(1)}, u32[]{:S(2)}, u32[]{:S(2)}) collective-permute-start(bf16[4,128,512]{2,1,0:T(8,128)(2,1)S(1)} %get-tuple-element.142), channel_id=1, source_target_pairs={{0,16},{8,24},{16,0},{24,8},{1,17},{9,25},{17,1},{25,9},{2,18},{10... | collective-permute-start | bytes 1572872 | tf_op jit(solution)/shard_map/ppermute | solution.py:67
  422.6 24.3 %collective-permute-start.79 = (bf16[128,512]{1,0:T(8,128)(2,1)S(1)}, bf16[128,512]{1,0:T(8,128)(2,1)S(1)}, u32[]{:S(2)}, u32[]{:S(2)}) collective-permute-start(bf16[128,512]{1,0:T(8,128)(2,1)S(1)} %get-tuple-element.183), channel_id=1, source_target_pairs={{0,2},{1,3},{2,0},{3,1},{4,6},{5,7},{6,4},{7,5},{8,10},{9,11},{10,... | collective-permute-start | bytes 393224 | tf_op jit(solution)/shard_map/ppermute | solution.py:67
  422.9 24.5 %collective-permute-start.81 = (bf16[128,512]{1,0:T(8,128)(2,1)S(1)}, bf16[128,512]{1,0:T(8,128)(2,1)S(1)}, u32[]{:S(2)}, u32[]{:S(2)}) collective-permute-start(bf16[128,512]{1,0:T(8,128)(2,1)S(1)} %get-tuple-element.184), channel_id=1, source_target_pairs={{0,6},{1,7},{2,4},{3,5},{4,2},{5,3},{6,0},{7,1},{8,14},{9,15},{10,... | collective-permute-start | bytes 393224 | tf_op jit(solution)/shard_map/ppermute | solution.py:67
  430.4 17.0 %collective-permute-start.80 = (bf16[128,512]{1,0:T(8,128)(2,1)S(1)}, bf16[128,512]{1,0:T(8,128)(2,1)S(1)}, u32[]{:S(2)}, u32[]{:S(2)}) collective-permute-start(bf16[128,512]{1,0:T(8,128)(2,1)S(1)} %get-tuple-element.185), channel_id=1, source_target_pairs={{0,4},{1,5},{2,6},{3,7},{4,0},{5,1},{6,2},{7,3},{8,12},{9,13},{10,... | collective-permute-start | bytes 393224 | tf_op jit(solution)/shard_map/ppermute | solution.py:67
  444.5 11.4 %collective-permute-start.61 = (bf16[128,512]{1,0:T(8,128)(2,1)S(1)}, bf16[128,512]{1,0:T(8,128)(2,1)S(1)}, u32[]{:S(2)}, u32[]{:S(2)}) collective-permute-start(bf16[128,512]{1,0:T(8,128)(2,1)S(1)} %get-tuple-element.191), channel_id=1, source_target_pairs={{0,6},{1,7},{2,4},{3,5},{4,2},{5,3},{6,0},{7,1},{8,14},{9,15},{10,... | collective-permute-start | bytes 393224 | tf_op jit(solution)/shard_map/ppermute | solution.py:67
  446.9 21.1 %collective-permute-start.60 = (bf16[128,512]{1,0:T(8,128)(2,1)S(1)}, bf16[128,512]{1,0:T(8,128)(2,1)S(1)}, u32[]{:S(2)}, u32[]{:S(2)}) collective-permute-start(bf16[128,512]{1,0:T(8,128)(2,1)S(1)} %get-tuple-element.192), channel_id=1, source_target_pairs={{0,4},{1,5},{2,6},{3,7},{4,0},{5,1},{6,2},{7,3},{8,12},{9,13},{10,... | collective-permute-start | bytes 393224 | tf_op jit(solution)/shard_map/ppermute | solution.py:67
  447.5 24.0 %collective-permute-start.84 = (bf16[128,512]{1,0:T(8,128)(2,1)S(1)}, bf16[128,512]{1,0:T(8,128)(2,1)S(1)}, u32[]{:S(2)}, u32[]{:S(2)}) collective-permute-start(bf16[128,512]{1,0:T(8,128)(2,1)S(1)} %fusion.39), channel_id=1, source_target_pairs={{0,2},{1,3},{2,0},{3,1},{4,6},{5,7},{6,4},{7,5},{8,10},{9,11},{10,... | collective-permute-start | bytes 393224 | tf_op jit(solution)/shard_map/ppermute | solution.py:67
  449.1 23.4 %collective-permute-start.83 = (bf16[128,512]{1,0:T(8,128)(2,1)S(1)}, bf16[128,512]{1,0:T(8,128)(2,1)S(1)}, u32[]{:S(2)}, u32[]{:S(2)}) collective-permute-start(bf16[128,512]{1,0:T(8,128)(2,1)S(1)} %fusion.39), channel_id=1, source_target_pairs={{0,4},{1,5},{2,6},{3,7},{4,0},{5,1},{6,2},{7,3},{8,12},{9,13},{10,... | collective-permute-start | bytes 393224 | tf_op jit(solution)/shard_map/ppermute | solution.py:67
  452.0 20.5 %collective-permute-start.82 = (bf16[128,512]{1,0:T(8,128)(2,1)S(1)}, bf16[128,512]{1,0:T(8,128)(2,1)S(1)}, u32[]{:S(2)}, u32[]{:S(2)}) collective-permute-start(bf16[128,512]{1,0:T(8,128)(2,1)S(1)} %fusion.39), channel_id=1, source_target_pairs={{0,6},{1,7},{2,4},{3,5},{4,2},{5,3},{6,0},{7,1},{8,14},{9,15},{10,... | collective-permute-start | bytes 393224 | tf_op jit(solution)/shard_map/ppermute | solution.py:67
  468.1 11.1 %collective-permute-start.63 = (bf16[128,512]{1,0:T(8,128)(2,1)S(1)}, bf16[128,512]{1,0:T(8,128)(2,1)S(1)}, u32[]{:S(2)}, u32[]{:S(2)}) collective-permute-start(bf16[128,512]{1,0:T(8,128)(2,1)S(1)} %fusion.42), channel_id=1, source_target_pairs={{0,4},{1,5},{2,6},{3,7},{4,0},{5,1},{6,2},{7,3},{8,12},{9,13},{10,... | collective-permute-start | bytes 393224 | tf_op jit(solution)/shard_map/ppermute | solution.py:67
  473.5 31.1 %collective-permute-start.91 = (bf16[512,512]{1,0:T(8,128)(2,1)S(1)}, bf16[512,512]{1,0:T(8,128)(2,1)}, u32[]{:S(2)}, u32[]{:S(2)}) collective-permute-start(bf16[512,512]{1,0:T(8,128)(2,1)S(1)} %get-tuple-element.126), channel_id=1, source_target_pairs={{0,1},{1,0},{2,3},{3,2},{4,5},{5,4},{6,7},{7,6},{8,9},{9,8},{10,11... | collective-permute-start | bytes 1572872 | tf_op jit(solution)/shard_map/ppermute | solution.py:67
  483.1 22.7 %collective-permute-start.92 = (bf16[512,512]{1,0:T(8,128)(2,1)S(1)}, bf16[512,512]{1,0:T(8,128)(2,1)}, u32[]{:S(2)}, u32[]{:S(2)}) collective-permute-start(bf16[512,512]{1,0:T(8,128)(2,1)S(1)} %get-tuple-element.130), channel_id=1, source_target_pairs={{0,1},{1,0},{2,3},{3,2},{4,5},{5,4},{6,7},{7,6},{8,9},{9,8},{10,11... | collective-permute-start | bytes 1572872 | tf_op jit(solution)/shard_map/ppermute | solution.py:67
  484.2 10.4 %collective-permute-start.88 = (f32[1,1]{1,0:T(1,128)}, f32[1,1]{1,0:T(1,128)}, u32[]{:S(2)}, u32[]{:S(2)}) collective-permute-start(f32[1,1]{1,0:T(1,128)} %add.531), channel_id=1, source_target_pairs={{0,24},{8,16},{16,8},{24,0},{1,25},{9,17},{17,9},{25,1},{2,26},{10... | collective-permute-start | bytes 20 | tf_op jit(solution)/shard_map/ppermute | solution.py:67
  (83 other events, 713.3 us)
